TPU v7x, 128 devices: a whole 4x4x4 slice. The times are simulated.
128 devices in a mesh: brick: 8 (over y, core), grp: 16 (over x, z).
Axes of the slice: x: 4, y: 4, z: 4, core: 2. Of those that a mesh axis runs over, the one named last changes fastest.
Arguments:
- source: float32 [16, 8, 2, 32, 1024], P('grp', 'brick'), may hold values from -21 to 21
- uptake: float32 [16, 8, 2, 32, 1024], P('grp', 'brick'), may hold values from 0.00015 to 0.006
- conductance: float32 [16, 8, 6, 2, 32, 1024], P('grp', 'brick'), may hold values from 0 to 3, as said below
- occupancy: int32 [16, 2, 8], replicated, may hold values from 0 to 1, as said below
- assignment: int32 [8], replicated, may hold values from 0 to 7, as said below
Outputs:
- solution_field: float32 [16, 8, 2, 32, 1024], P('grp', 'brick')
- residual: float32 [16, 8, 2, 32, 1024], P('grp', 'brick')
Inputs may be any that keep to these rules, and one draw needn't show every extreme that they name: `occupancy`: 1 marks an occupied brick; in every draw one patch of some slab has all its bricks occupied. `assignment`: each patch is held by exactly one index of brick. `conductance`: equal at both ends of a bond: the value toward +x at a cell is the value toward -x at its +x neighbour, likewise for y and z, the lattice being read cyclically; values toward +z and -z are 0.3 or more.
All inputs are finite; a program needn't handle non-finite values.
Results may differ from a plain program's by a relative error of at most 0.0003.
Values sent between devices are 32-bit elements; how exact they have to be, the bound alone decides.
A program may use at most 128 MiB of HBM per device.

v0:
```python
import jax
import jax.numpy as jnp
from jax import lax
from jax.sharding import PartitionSpec as P

BS = 32
PATCH_X = 1
PATCH_Y = 2
ITERS = 3


OMEGA = 0.6


def extended_2(block, sides, width):
    for axis, dim in sides:
        count = lax.axis_size(axis)
        forward = [(i, i + 1) for i in range(count - 1)]
        backward = [(target, source) for source, target in forward]
        low = lax.ppermute(
            lax.slice_in_dim(block, block.shape[dim] - width, None, axis=dim), axis, forward
        )
        high = lax.ppermute(lax.slice_in_dim(block, 0, width, axis=dim), axis, backward)
        block = jnp.concatenate([low, block, high], axis=dim)
    return block


def assemble(coarse_diag, couplings, strides):
    extent = coarse_diag.shape[0]
    matrix = jnp.diag(coarse_diag)
    for coupling, stride in zip(couplings, strides):
        banded = coupling[: extent - stride]
        matrix = matrix - jnp.diag(banded, stride) - jnp.diag(banded, -stride)
    return matrix


def pad_rows(block, capacity):
    return jnp.pad(block, ((0, capacity - block.shape[0]), (0, 0)))


def on_device(source, uptake, conductance, occupancy, assignment):
    face_size = BS * BS
    capacity = max(PATCH_X, PATCH_Y)
    slot_count = PATCH_X * PATCH_Y
    slab_index = lax.axis_index("grp")
    brick_index = lax.axis_index("brick")
    brick_count = lax.axis_size("brick")
    across = brick_count // 2
    peer_ids = jnp.arange(brick_count, dtype=jnp.int32)
    patch_index = assignment[brick_index]
    patch_row = patch_index // across
    patch_column = patch_index % across

    def owner_of(row_shift, column_shift):
        row_target = patch_row + row_shift
        column_target = patch_column + column_shift
        inside = (
            (row_target >= 0) & (row_target < 2) & (column_target >= 0) & (column_target < across)
        )
        holder = jnp.sum(jnp.where(assignment == row_target * across + column_target, peer_ids, 0))
        return jnp.where(inside, holder, -1)

    wanted = jnp.stack([owner_of(1, 0), owner_of(-1, 0), owner_of(0, 1), owner_of(0, -1)])
    padded = jnp.pad(occupancy, 1)
    window = lax.dynamic_slice(
        padded,
        (slab_index, patch_row * PATCH_X, patch_column * PATCH_Y),
        (3, PATCH_X + 2, PATCH_Y + 2),
    ).astype(jnp.float32)
    centre = window[1, 1:-1, 1:-1].reshape(slot_count)
    toward = [
        window[1, 2:, 1:-1],
        window[1, :-2, 1:-1],
        window[1, 1:-1, 2:],
        window[1, 1:-1, :-2],
        window[2, 1:-1, 1:-1],
        window[0, 1:-1, 1:-1],
    ]
    first_axis = lax.broadcasted_iota(jnp.int32, (1, BS, face_size), 1)
    flat_axis = lax.broadcasted_iota(jnp.int32, (1, BS, face_size), 2)
    second_axis = flat_axis // BS
    third_axis = flat_axis % BS
    cube_third = lax.broadcasted_iota(jnp.int32, (1, BS, BS, BS), 3)
    borders = [
        first_axis == BS - 1,
        first_axis == 0,
        second_axis == BS - 1,
        second_axis == 0,
        third_axis == BS - 1,
        third_axis == 0,
    ]
    bonds = conductance[0, 0]
    live_here = centre[:, None, None]
    effective = []
    for direction in range(6):
        neighbour_live = toward[direction].reshape(slot_count)[:, None, None]
        active = jnp.where(borders[direction], live_here * neighbour_live, live_here)
        effective.append(bonds[direction] * active)
    absorb = uptake[0, 0]
    diagonal = absorb
    for direction in range(6):
        diagonal = diagonal + effective[direction]

    def apply_operator(field):
        lower_x = field[:, 0, :]
        upper_x = field[:, BS - 1, :]
        lower_y = field[:, :, :BS].reshape(slot_count, face_size)
        upper_y = field[:, :, face_size - BS :].reshape(slot_count, face_size)
        cube = field.reshape(slot_count, BS, BS, BS)
        lower_z = cube[:, :, :, 0].reshape(slot_count, face_size)
        upper_z = cube[:, :, :, BS - 1].reshape(slot_count, face_size)
        grid_lower_x = lower_x.reshape(PATCH_X, PATCH_Y, face_size)
        grid_upper_x = upper_x.reshape(PATCH_X, PATCH_Y, face_size)
        grid_lower_y = lower_y.reshape(PATCH_X, PATCH_Y, face_size)
        grid_upper_y = upper_y.reshape(PATCH_X, PATCH_Y, face_size)
        outgoing_sides = jnp.stack(
            [
                pad_rows(grid_lower_x[0], capacity),
                pad_rows(grid_upper_x[PATCH_X - 1], capacity),
                pad_rows(grid_lower_y[:, 0], capacity),
                pad_rows(grid_upper_y[:, PATCH_Y - 1], capacity),
            ]
        )
        portion = lax.all_gather(outgoing_sides[None], "brick", axis=0, tiled=True)
        sources = jnp.arange(portion.shape[0], dtype=jnp.int32)
        matches = sources[:, None] == wanted[None, :]
        remote = jnp.zeros((4, capacity, face_size), jnp.float32) + jnp.sum(
            jnp.where(matches[:, :, None, None], portion, 0.0), axis=0
        )
        stacked = jnp.stack([lower_z, upper_z])
        extended = extended_2(stacked, (("grp", 0),), 1)
        from_below = extended[0].reshape(slot_count, BS, BS, 1)
        from_above = extended[3].reshape(slot_count, BS, BS, 1)
        beyond_xplus = jnp.concatenate(
            [grid_lower_x[1:], remote[0, :PATCH_Y][None]], axis=0
        ).reshape(slot_count, face_size)
        beyond_xminus = jnp.concatenate(
            [remote[1, :PATCH_Y][None], grid_upper_x[:-1]], axis=0
        ).reshape(slot_count, face_size)
        beyond_yplus = jnp.concatenate(
            [grid_lower_y[:, 1:], remote[2, :PATCH_X][:, None]], axis=1
        ).reshape(slot_count, BS, BS)
        beyond_yminus = jnp.concatenate(
            [remote[3, :PATCH_X][:, None], grid_upper_y[:, :-1]], axis=1
        ).reshape(slot_count, BS, BS)
        upper_neighbour = jnp.where(
            cube_third == BS - 1, from_above, jnp.roll(cube, -1, axis=3)
        ).reshape(slot_count, BS, face_size)
        lower_neighbour = jnp.where(cube_third == 0, from_below, jnp.roll(cube, 1, axis=3)).reshape(
            slot_count, BS, face_size
        )
        total = diagonal * field
        total = total - effective[0] * jnp.concatenate(
            [field[:, 1:, :], beyond_xplus[:, None, :]], axis=1
        )
        total = total - effective[1] * jnp.concatenate(
            [beyond_xminus[:, None, :], field[:, :-1, :]], axis=1
        )
        total = total - effective[2] * jnp.concatenate([field[:, :, BS:], beyond_yplus], axis=2)
        total = total - effective[3] * jnp.concatenate(
            [beyond_yminus, field[:, :, : face_size - BS]], axis=2
        )
        total = total - effective[4] * upper_neighbour
        total = total - effective[5] * lower_neighbour
        return total

    slot_ids = jnp.arange(slot_count)
    brick_first = slot_ids // PATCH_Y
    brick_second = slot_ids % PATCH_Y
    inside = [
        (brick_first < PATCH_X - 1).astype(jnp.float32),
        (brick_first > 0).astype(jnp.float32),
        (brick_second < PATCH_Y - 1).astype(jnp.float32),
        (brick_second > 0).astype(jnp.float32),
    ]
    face_sums = [
        jnp.sum(effective[0][:, BS - 1, :], axis=1),
        jnp.sum(effective[1][:, 0, :], axis=1),
        jnp.sum(effective[2][:, :, face_size - BS :], axis=(1, 2)),
        jnp.sum(effective[3][:, :, :BS], axis=(1, 2)),
        jnp.sum(effective[4].reshape(slot_count, BS, BS, BS)[:, :, :, BS - 1], axis=(1, 2)),
        jnp.sum(effective[5].reshape(slot_count, BS, BS, BS)[:, :, :, 0], axis=(1, 2)),
    ]
    coarse_diag = jnp.sum(absorb, axis=(1, 2))
    for direction in range(4):
        coarse_diag = coarse_diag + face_sums[direction] * inside[direction]
    coarse_diag = coarse_diag + face_sums[4] + face_sums[5]
    record = jnp.stack(
        [coarse_diag, face_sums[0] * inside[0], face_sums[2] * inside[2], face_sums[4]]
    )[None]
    gathered = lax.all_gather(record, "grp", axis=0, tiled=True)
    columns = jnp.transpose(gathered, (1, 0, 2)).reshape(4, -1)
    matrix = assemble(columns[0], (columns[1], columns[2], columns[3]), (PATCH_Y, 1, slot_count))
    factor = jnp.linalg.cholesky(matrix)

    def coarse_solve(residual_field):
        totals = jnp.sum(residual_field, axis=(1, 2))
        gathered_terms = lax.all_gather(totals[None], "grp", axis=0, tiled=True).reshape(-1, 1)
        middle = lax.linalg.triangular_solve(factor, gathered_terms, left_side=True, lower=True)
        result = lax.linalg.triangular_solve(
            factor, middle, left_side=True, lower=True, transpose_a=True
        )
        return lax.dynamic_slice_in_dim(result[:, 0], slab_index * slot_count, slot_count)

    def precondition(residual_field):
        smoothed = OMEGA * residual_field / diagonal
        smoothed = smoothed + OMEGA * (residual_field - apply_operator(smoothed)) / diagonal
        return smoothed + coarse_solve(residual_field)[:, None, None]

    forcing = source[0, 0] * live_here
    solution_field = jnp.zeros_like(forcing)
    residual = forcing

    def global_sum(values):
        return lax.psum(jnp.sum(values), ("brick", "grp"))

    search = precondition(residual)
    energy = global_sum(residual * search)
    for iteration in range(ITERS):
        mapped = apply_operator(search)
        step_size = energy / global_sum(search * mapped)
        solution_field = solution_field + step_size * search
        residual = residual - step_size * mapped
        if iteration + 1 < ITERS:
            smoothed = precondition(residual)
            renewed = global_sum(residual * smoothed)
            search = smoothed + renewed / energy * search
            energy = renewed
    return (solution_field[None, None], residual[None, None])


def solution(mesh):
    return jax.shard_map(
        on_device,
        mesh=mesh,
        in_specs=(
            P("grp", "brick", None, None, None),
            P("grp", "brick", None, None, None),
            P("grp", "brick", None, None, None, None),
            P(),
            P(),
        ),
        out_specs=(P("grp", "brick", None, None, None), P("grp", "brick", None, None, None)),
        check_vma=False,
    )
```

profile of v0, /device:TPU:0, one launch (start us, length us, event | category | flops | bytes accessed | tf_op | source)
XLA Modules:
  0.0 1063.0 jit_solution(14409875242148923339)
XLA Ops:
  15.4 2.4 squeeze.120
  22.2 5.7 multiply_divide_fusion.2
  30.5 4.5 collective-permute-start.1
  45.2 13.4 %all-gather = f32[32,2,1024]{2,1,0:T(2,128)S(1)} all-gather(f32[4,2,1024]{2,1,0:T(2,128)S(1)} %copy.294), channel_id=2, replica_groups=mesh['brick'=8,'grp'=16] {'brick'}, dimensions={0}, use_global_device_ids=true | all-gather | bytes 294912 | tf_op jit(solution)/shard_map/all_gather | solution.py:124
  67.4 25.4 %all-gather.10 = f32[16,4,2]{1,2,0:T(2,128)S(1)} all-gather(f32[1,4,2]{1,2,0:T(2,128)S(1)} %bitcast.616), channel_id=3, replica_groups=mesh['brick'=8,'grp'=16] {'grp'}, dimensions={0}, use_global_device_ids=true | all-gather | bytes 544 | tf_op jit(solution)/shard_map/all_gather | solution.py:191
  98.4 38.3 %all-reduce.18 = f32[32]{0:T(128)S(1)} all-reduce(f32[32]{0:T(128)S(1)} %dynamic-update-slice.3), channel_id=4, replica_groups=mesh['brick'=8,'grp'=16] {'grp'}, use_global_device_ids=true, to_apply=%add.18 | all-reduce | flops 32 | bytes 256 | tf_op jit(solution)/shard_map/triangular_solve/reshape.87 | solution.py:199
  141.8 2.9 cholesky.19
  146.1 2.4 custom-call.14
  164.6 8.4 fusion.46
  173.1 2.4 concatenate.643
  175.5 2.4 concatenate.645
  179.2 2.4 broadcast_in_dim.696
  183.0 2.4 broadcast_in_dim.702
  196.1 12.8 %all-gather.3 = f32[32,2,1024]{2,1,0:T(2,128)S(1)} all-gather(f32[4,2,1024]{2,1,0:T(2,128)S(1)} %copy.298), channel_id=5, replica_groups=mesh['brick'=8,'grp'=16] {'brick'}, dimensions={0}, use_global_device_ids=true | all-gather | bytes 294912 | tf_op jit(solution)/shard_map/all_gather | solution.py:124
  224.9 3.0 pad_maximum_fusion.2
  229.9 2.4 concatenate.676
  232.3 2.4 concatenate.677
  234.7 2.4 broadcast_in_dim.743
  250.5 2.4 concatenate.726
  257.7 2.4 concatenate.663
  270.5 2.4 broadcast_in_dim.729
  276.4 2.4 broadcast_in_dim.761
  278.8 2.4 broadcast_in_dim.726
  281.2 3.7 multiply_reduce_fusion.3
  285.0 64.5 %all-reduce.21 = (f32[]{:T(128)}, f32[]{:T(128)}) all-reduce(f32[]{:T(128)} %get-tuple-element.21, f32[]{:T(128)} %get-tuple-element.20), channel_id=1, replica_groups=mesh['brick'=8,'grp'=16] {'brick','grp'}, use_global_device_ids=true, to_apply=%region_16.19 | all-reduce | flops 2 | bytes 16 | tf_op jit(solution)/shard_map/psum | solution.py:215
  361.2 13.0 %all-gather.4 = f32[32,2,1024]{2,1,0:T(2,128)S(1)} all-gather(f32[4,2,1024]{2,1,0:T(2,128)S(1)} %copy.304), channel_id=6, replica_groups=mesh['brick'=8,'grp'=16] {'brick'}, dimensions={0}, use_global_device_ids=true | all-gather | bytes 294912 | tf_op jit(solution)/shard_map/all_gather | solution.py:124
  384.0 9.1 multiply_divide_fusion.1
  399.0 38.7 %all-reduce.19 = f32[32]{0:T(128)} all-reduce(f32[32]{0:T(128)} %dynamic-update-slice.4), channel_id=7, replica_groups=mesh['brick'=8,'grp'=16] {'grp'}, use_global_device_ids=true, to_apply=%add.19 | all-reduce | flops 32 | bytes 256 | tf_op jit(solution)/shard_map/triangular_solve/reshape.87 | solution.py:199
  447.8 3.0 pad_maximum_fusion.4
  453.2 3.0 fusion.96
  484.7 2.4 broadcast_in_dim.752
  493.0 3.7 multiply_reduce_fusion.2
  496.7 64.8 %psum.44 = f32[]{:T(128)} all-reduce(f32[]{:T(128)} %get-tuple-element.54), channel_id=1, replica_groups=mesh['brick'=8,'grp'=16] {'brick','grp'}, use_global_device_ids=true, to_apply=%region_23.26 | all-reduce | flops 1 | bytes 8 | tf_op jit(solution)/shard_map/psum | solution.py:215
  565.4 12.8 %all-gather.6 = f32[32,2,1024]{2,1,0:T(2,128)S(1)} all-gather(f32[4,2,1024]{2,1,0:T(2,128)S(1)} %copy.309), channel_id=8, replica_groups=mesh['brick'=8,'grp'=16] {'brick'}, dimensions={0}, use_global_device_ids=true | all-gather | bytes 294912 | tf_op jit(solution)/shard_map/all_gather | solution.py:124
  586.7 7.3 multiply_add_fusion.1
  598.6 2.5 collective-permute-start.7
  602.5 2.7 pad_maximum_fusion.6
  606.5 2.5 broadcast_in_dim.764
  609.0 2.4 broadcast_in_dim.763
  619.2 2.5 concatenate.791
  629.4 2.5 broadcast_in_dim.760
  636.4 3.3 multiply_reduce_fusion.1
  639.7 66.3 %psum.45 = f32[]{:T(128)} all-reduce(f32[]{:T(128)} %get-tuple-element.50), channel_id=1, replica_groups=mesh['brick'=8,'grp'=16] {'brick','grp'}, use_global_device_ids=true, to_apply=%region_26.29 | all-reduce | flops 1 | bytes 8 | tf_op jit(solution)/shard_map/psum | solution.py:215
  710.6 13.0 %all-gather.7 = f32[32,2,1024]{2,1,0:T(2,128)S(1)} all-gather(f32[4,2,1024]{2,1,0:T(2,128)S(1)} %copy.314), channel_id=9, replica_groups=mesh['brick'=8,'grp'=16] {'brick'}, dimensions={0}, use_global_device_ids=true | all-gather | bytes 294912 | tf_op jit(solution)/shard_map/all_gather | solution.py:124
  732.5 8.2 multiply_divide_fusion
  746.6 38.6 %all-reduce.20 = f32[32]{0:T(128)} all-reduce(f32[32]{0:T(128)} %dynamic-update-slice.5), channel_id=10, replica_groups=mesh['brick'=8,'grp'=16] {'grp'}, use_global_device_ids=true, to_apply=%add.20 | all-reduce | flops 32 | bytes 256 | tf_op jit(solution)/shard_map/triangular_solve/reshape.87 | solution.py:199
  793.9 3.0 pad_maximum_fusion.8
  811.8 2.4 concatenate.804
  816.6 2.4 concatenate.805
  819.0 2.4 concatenate.759
  829.4 2.4 broadcast_in_dim.771
  835.3 2.4 broadcast_in_dim.768
  837.8 3.8 multiply_reduce_fusion
  841.6 64.8 %psum.46 = f32[]{:T(128)} all-reduce(f32[]{:T(128)} %get-tuple-element.42), channel_id=1, replica_groups=mesh['brick'=8,'grp'=16] {'brick','grp'}, use_global_device_ids=true, to_apply=%region_30.33 | all-reduce | flops 1 | bytes 8 | tf_op jit(solution)/shard_map/psum | solution.py:215
  914.3 12.8 %all-gather.9 = f32[32,2,1024]{2,1,0:T(2,128)S(1)} all-gather(f32[4,2,1024]{2,1,0:T(2,128)S(1)} %copy.319), channel_id=11, replica_groups=mesh['brick'=8,'grp'=16] {'brick'}, dimensions={0}, use_global_device_ids=true | all-gather | bytes 294912 | tf_op jit(solution)/shard_map/all_gather | solution.py:124
  936.9 10.7 %multiply_add_fusion = f32[2,32,32,32]{3,2,1,0:T(8,128)S(1)} fusion(f32[2,32,32,32]{3,2,1,0:T(8,128)} %copy-done.5, f32[2,32,32,32]{3,2,1,0:T(8,128)} %get-tuple-element.75, f32[2,32,32,32]{3,2,1,0:T(8,128)} %get-tuple-element.77, f32[2,32,32,32]{3,2,1,0:T(8,128)} %get-tuple-element.76, f32[2,32,32,32]{3,2,1,0:T(8,128)} %concatenate.773, ...), kind=kLoop, calls=%fused_computation.76 | loop fusion | flops 3735552 | bytes 5865592 | tf_op jit(solution)/shard_map/add | solution.py:227
  958.3 2.4 broadcast_in_dim.783
  960.7 2.4 broadcast_in_dim.782
  965.9 2.4 concatenate.818
  968.3 2.4 concatenate.775
  977.0 2.5 broadcast_in_dim.779
  983.3 2.6 fusion.155
  987.6 66.7 %psum.47 = f32[]{:T(128)} all-reduce(f32[]{:T(128)} %fusion.155), channel_id=1, replica_groups=mesh['brick'=8,'grp'=16] {'brick','grp'}, use_global_device_ids=true, to_apply=%region_33.36 | all-reduce | flops 1 | bytes 8 | tf_op jit(solution)/shard_map/psum | solution.py:215
  1055.7 6.0 fusion.149
  (697 shorter events, 333.4 us)
Async XLA Ops:
  0.6 9.8 copy-start.37
  0.6 11.2 %copy-start = (f32[1,1,6,2,32,1024]{5,4,3,2,1,0:T(8,128)S(1)}, f32[1,1,6,2,32,1024]{5,4,3,2,1,0:T(8,128)}, u32[]{:S(2)}) copy-start(f32[1,1,6,2,32,1024]{5,4,3,2,1,0:T(8,128)} %param.11) | copy-start | bytes 4718596
  4.7 34.4 %copy-start.95 = (pred[32]{0:T(512)(128)(4,1)}, pred[32]{0:T(512)(128)(4,1)S(1)}, u32[]{:S(2)}) copy-start(pred[32]{0:T(512)(128)(4,1)S(1)} %get-tuple-element.277) | copy-start | bytes 100
  4.7 34.4 %copy-start.101 = (pred[32]{0:T(512)(128)(4,1)}, pred[32]{0:T(512)(128)(4,1)S(1)}, u32[]{:S(2)}) copy-start(pred[32]{0:T(512)(128)(4,1)S(1)} %get-tuple-element.278) | copy-start | bytes 100
  8.2 30.9 %copy-start.85 = (f32[2]{0:T(128)}, f32[2]{0:T(128)S(1)}, u32[]{:S(2)}) copy-start(f32[2]{0:T(128)S(1)} %get-tuple-element.32) | copy-start | bytes 28
  15.3 6.9 copy-start.1
  22.2 16.9 %copy-start.118 = (f32[2]{0:T(128)}, f32[2]{0:T(128)S(1)}, u32[]{:S(2)}) copy-start(f32[2]{0:T(128)S(1)} %get-tuple-element.268) | copy-start | bytes 28
  27.9 10.2 copy-start.20
  28.0 11.1 %copy-start.38 = (f32[1,1,2,32,1024]{4,3,2,1,0:T(8,128)S(1)}, f32[1,1,2,32,1024]{4,3,2,1,0:T(8,128)}, u32[]{:S(2)}) copy-start(f32[1,1,2,32,1024]{4,3,2,1,0:T(8,128)} %param.10) | copy-start | bytes 786436
  28.0 11.1 %copy-start.122 = (f32[2]{0:T(128)S(1)}, f32[2]{0:T(128)}, u32[]{:S(2)}) copy-start(f32[2]{0:T(128)} %copy-done.121) | copy-start | bytes 28
  28.0 11.1 %copy-start.125 = (f32[2]{0:T(128)S(1)}, f32[2]{0:T(128)}, u32[]{:S(2)}) copy-start(f32[2]{0:T(128)} %copy-done.124) | copy-start | bytes 28
  28.0 11.1 %copy-start.130 = (f32[2]{0:T(128)S(1)}, f32[2]{0:T(128)}, u32[]{:S(2)}) copy-start(f32[2]{0:T(128)} %copy-done.129) | copy-start | bytes 28
  28.0 11.1 %copy-start.134 = (f32[2]{0:T(128)S(1)}, f32[2]{0:T(128)}, u32[]{:S(2)}) copy-start(f32[2]{0:T(128)} %copy-done.133) | copy-start | bytes 28
  28.0 11.1 %copy-start.138 = (f32[2]{0:T(128)S(1)}, f32[2]{0:T(128)}, u32[]{:S(2)}) copy-start(f32[2]{0:T(128)} %copy-done.137) | copy-start | bytes 28
  30.5 133.3 %collective-permute-start.1 = (f32[1,2,1024]{2,1,0:T(2,128)}, f32[1,2,1024]{2,1,0:T(2,128)}, u32[]{:S(2)}, u32[]{:S(2)}) collective-permute-start(f32[1,2,1024]{2,1,0:T(2,128)} %stack_reshape_squeeze.37), channel_id=1, source_target_pairs={{0,1},{1,2},{2,3},{3,4},{4,5},{5,6},{6,7},{7,8},{8,9},{9,10},{10,1... | collective-permute-start | bytes 24584 | tf_op jit(solution)/shard_map/ppermute | solution.py:20
  35.6 127.4 %collective-permute-start = (f32[1,2,1024]{2,1,0:T(2,128)}, f32[1,2,1024]{2,1,0:T(2,128)}, u32[]{:S(2)}, u32[]{:S(2)}) collective-permute-start(f32[1,2,1024]{2,1,0:T(2,128)} %stack_reshape_squeeze.36), channel_id=1, source_target_pairs={{1,0},{2,1},{3,2},{4,3},{5,4},{6,5},{7,6},{8,7},{9,8},{10,9},{11,1... | collective-permute-start | bytes 24584 | tf_op jit(solution)/shard_map/ppermute | solution.py:23
  40.2 19.2 %copy-start.31 = (f32[2,32,1024]{2,1,0:T(8,128)}, f32[2,32,1024]{2,1,0:T(8,128)S(1)}, u32[]{:S(2)}) copy-start(f32[2,32,1024]{2,1,0:T(8,128)S(1)} %get-tuple-element.68) | copy-start | bytes 786436
  40.2 26.2 %copy-start.13 = (f32[2,32,1024]{2,1,0:T(8,128)}, f32[2,32,1024]{2,1,0:T(8,128)S(1)}, u32[]{:S(2)}) copy-start(f32[2,32,1024]{2,1,0:T(8,128)S(1)} %get-tuple-element.73) | copy-start | bytes 786436
  40.3 452.7 %copy-start.11 = (f32[2,32,1024]{2,1,0:T(8,128)}, f32[2,32,1024]{2,1,0:T(8,128)S(1)}, u32[]{:S(2)}) copy-start(f32[2,32,1024]{2,1,0:T(8,128)S(1)} %get-tuple-element.72) | copy-start | bytes 786436
  43.7 15.6 %copy-start.141 = (pred[8,4]{1,0:T(8,128)(4,1)}, pred[8,4]{1,0:T(8,128)(4,1)S(1)}, u32[]{:S(2)}) copy-start(pred[8,4]{1,0:T(8,128)(4,1)S(1)} %iota_compare_fusion.11) | copy-start | bytes 100
  60.0 6.6 copy-start.3
  67.0 26.8 %copy-start.7 = (f32[2,32,32,32]{3,2,1,0:T(8,128)S(1)}, f32[2,32,32,32]{3,2,1,0:T(8,128)}, u32[]{:S(2)}) copy-start(f32[2,32,32,32]{3,2,1,0:T(8,128)} %copy-done.6) | copy-start | bytes 786436
  93.7 55.1 %copy-start.59 = (f32[2,32,992]{2,1,0:T(8,128)S(1)}, f32[2,32,992]{2,1,0:T(8,128)}, u32[]{:S(2)}) copy-start(f32[2,32,992]{2,1,0:T(8,128)} %get-tuple-element.146) | copy-start | bytes 761860
  95.5 60.8 %copy-start.96 = (pred[32]{0:T(512)(128)(4,1)S(1)}, pred[32]{0:T(512)(128)(4,1)}, u32[]{:S(2)}) copy-start(pred[32]{0:T(512)(128)(4,1)} %copy-done.95) | copy-start | bytes 100
  95.5 61.4 %copy-start.102 = (pred[32]{0:T(512)(128)(4,1)S(1)}, pred[32]{0:T(512)(128)(4,1)}, u32[]{:S(2)}) copy-start(pred[32]{0:T(512)(128)(4,1)} %copy-done.101) | copy-start | bytes 100
  137.5 22.8 %copy-start.81 = (f32[2,32,32]{2,1,0:T(8,128)}, f32[2,32,32]{2,1,0:T(8,128)S(1)}, u32[]{:S(2)}) copy-start(f32[2,32,32]{2,1,0:T(8,128)S(1)} %reshape.2206) | copy-start | bytes 24580
  138.3 22.1 %copy-start.82 = (f32[2,32,32]{2,1,0:T(8,128)}, f32[2,32,32]{2,1,0:T(8,128)S(1)}, u32[]{:S(2)}) copy-start(f32[2,32,32]{2,1,0:T(8,128)S(1)} %reshape.2205) | copy-start | bytes 24580
  148.9 11.5 %copy-start.57 = (f32[2,31,1024]{2,1,0:T(8,128)S(1)}, f32[2,31,1024]{2,1,0:T(8,128)}, u32[]{:S(2)}) copy-start(f32[2,31,1024]{2,1,0:T(8,128)} %get-tuple-element.142) | copy-start | bytes 761860
  150.1 14.4 %copy-start.156 = (f32[2]{0:T(128)}, f32[2]{0:T(128)S(1)}, u32[]{:S(2)}) copy-start(f32[2]{0:T(128)S(1)} %fusion.180) | copy-start | bytes 28
  220.0 44.6 %collective-permute-start.3 = (f32[1,2,1024]{2,1,0:T(2,128)}, f32[1,2,1024]{2,1,0:T(2,128)}, u32[]{:S(2)}, u32[]{:S(2)}) collective-permute-start(f32[1,2,1024]{2,1,0:T(2,128)} %stack_reshape_squeeze.39), channel_id=1, source_target_pairs={{0,1},{1,2},{2,3},{3,4},{4,5},{5,6},{6,7},{7,8},{8,9},{9,10},{10,1... | collective-permute-start | bytes 24584 | tf_op jit(solution)/shard_map/ppermute | solution.py:20
  221.9 51.0 %collective-permute-start.2 = (f32[1,2,1024]{2,1,0:T(2,128)}, f32[1,2,1024]{2,1,0:T(2,128)}, u32[]{:S(2)}, u32[]{:S(2)}) collective-permute-start(f32[1,2,1024]{2,1,0:T(2,128)} %stack_reshape_squeeze.38), channel_id=1, source_target_pairs={{1,0},{2,1},{3,2},{4,3},{5,4},{6,5},{7,6},{8,7},{9,8},{10,9},{11,1... | collective-permute-start | bytes 24584 | tf_op jit(solution)/shard_map/ppermute | solution.py:23
  359.0 19.4 %copy-start.34 = (f32[2,32,1024]{2,1,0:T(8,128)S(1)}, f32[2,32,1024]{2,1,0:T(8,128)}, u32[]{:S(2)}) copy-start(f32[2,32,1024]{2,1,0:T(8,128)} %copy-done.33) | copy-start | bytes 786436
  442.0 39.2 %collective-permute-start.5 = (f32[1,2,1024]{2,1,0:T(2,128)}, f32[1,2,1024]{2,1,0:T(2,128)}, u32[]{:S(2)}, u32[]{:S(2)}) collective-permute-start(f32[1,2,1024]{2,1,0:T(2,128)} %stack_reshape_squeeze.41), channel_id=1, source_target_pairs={{0,1},{1,2},{2,3},{3,4},{4,5},{5,6},{6,7},{7,8},{8,9},{9,10},{10,1... | collective-permute-start | bytes 24584 | tf_op jit(solution)/shard_map/ppermute | solution.py:20
  443.9 43.2 %collective-permute-start.4 = (f32[1,2,1024]{2,1,0:T(2,128)}, f32[1,2,1024]{2,1,0:T(2,128)}, u32[]{:S(2)}, u32[]{:S(2)}) collective-permute-start(f32[1,2,1024]{2,1,0:T(2,128)} %stack_reshape_squeeze.40), channel_id=1, source_target_pairs={{1,0},{2,1},{3,2},{4,3},{5,4},{6,5},{7,6},{8,7},{9,8},{10,9},{11,1... | collective-permute-start | bytes 24584 | tf_op jit(solution)/shard_map/ppermute | solution.py:23
  595.4 7.0 copy-start.8
  595.4 7.0 copy-start.151
  595.4 7.0 copy-start.153
  598.6 28.0 %collective-permute-start.7 = (f32[1,2,1024]{2,1,0:T(2,128)}, f32[1,2,1024]{2,1,0:T(2,128)}, u32[]{:S(2)}, u32[]{:S(2)}) collective-permute-start(f32[1,2,1024]{2,1,0:T(2,128)} %stack_reshape_squeeze.43), channel_id=1, source_target_pairs={{0,1},{1,2},{2,3},{3,4},{4,5},{5,6},{6,7},{7,8},{8,9},{9,10},{10,1... | collective-permute-start | bytes 24584 | tf_op jit(solution)/shard_map/ppermute | solution.py:20
  601.1 30.7 %collective-permute-start.6 = (f32[1,2,1024]{2,1,0:T(2,128)}, f32[1,2,1024]{2,1,0:T(2,128)}, u32[]{:S(2)}, u32[]{:S(2)}) collective-permute-start(f32[1,2,1024]{2,1,0:T(2,128)} %stack_reshape_squeeze.42), channel_id=1, source_target_pairs={{1,0},{2,1},{3,2},{4,3},{5,4},{6,5},{7,6},{8,7},{9,8},{10,9},{11,1... | collective-permute-start | bytes 24584 | tf_op jit(solution)/shard_map/ppermute | solution.py:23
  606.5 10.3 copy-start.22
  629.3 7.0 copy-start.12
  629.3 7.0 copy-start.14
  629.3 7.0 copy-start.16
  629.3 7.0 copy-start.18
  636.4 71.0 %copy-start.45 = (f32[2,32,1024]{2,1,0:T(8,128)S(1)}, f32[2,32,1024]{2,1,0:T(8,128)}, u32[]{:S(2)}) copy-start(f32[2,32,1024]{2,1,0:T(8,128)} %copy-done.44) | copy-start | bytes 786436
  709.0 17.8 %copy-start.54 = (f32[2,32,1024]{2,1,0:T(8,128)}, f32[2,32,1024]{2,1,0:T(8,128)S(1)}, u32[]{:S(2)}) copy-start(f32[2,32,1024]{2,1,0:T(8,128)S(1)} %get-tuple-element.47) | copy-start | bytes 786436
  789.3 36.6 %collective-permute-start.9 = (f32[1,2,1024]{2,1,0:T(2,128)}, f32[1,2,1024]{2,1,0:T(2,128)}, u32[]{:S(2)}, u32[]{:S(2)}) collective-permute-start(f32[1,2,1024]{2,1,0:T(2,128)} %stack_reshape_squeeze.45), channel_id=1, source_target_pairs={{0,1},{1,2},{2,3},{3,4},{4,5},{5,6},{6,7},{7,8},{8,9},{9,10},{10,1... | collective-permute-start | bytes 24584 | tf_op jit(solution)/shard_map/ppermute | solution.py:20
  791.2 40.6 %collective-permute-start.8 = (f32[1,2,1024]{2,1,0:T(2,128)}, f32[1,2,1024]{2,1,0:T(2,128)}, u32[]{:S(2)}, u32[]{:S(2)}) collective-permute-start(f32[1,2,1024]{2,1,0:T(2,128)} %stack_reshape_squeeze.44), channel_id=1, source_target_pairs={{1,0},{2,1},{3,2},{4,3},{5,4},{6,5},{7,6},{8,7},{9,8},{10,9},{11,1... | collective-permute-start | bytes 24584 | tf_op jit(solution)/shard_map/ppermute | solution.py:23
  829.4 8.3 copy-start.89
  829.4 8.3 copy-start.108
  829.4 8.3 copy-start.110
  829.4 8.3 copy-start.120
  912.9 18.4 %copy-start.36 = (f32[2,32,1024]{2,1,0:T(8,128)S(1)}, f32[2,32,1024]{2,1,0:T(8,128)}, u32[]{:S(2)}) copy-start(f32[2,32,1024]{2,1,0:T(8,128)} %copy-done.35) | copy-start | bytes 786436
  951.4 22.9 %collective-permute-start.11 = (f32[1,2,1024]{2,1,0:T(2,128)S(1)}, f32[1,2,1024]{2,1,0:T(2,128)S(1)}, u32[]{:S(2)}, u32[]{:S(2)}) collective-permute-start(f32[1,2,1024]{2,1,0:T(2,128)S(1)} %stack_reshape_squeeze.47), channel_id=1, source_target_pairs={{0,1},{1,2},{2,3},{3,4},{4,5},{5,6},{6,7},{7,8},{8,9},{9,10},{10,1... | collective-permute-start | bytes 24584 | tf_op jit(solution)/shard_map/ppermute | solution.py:20
  953.2 26.3 %collective-permute-start.10 = (f32[1,2,1024]{2,1,0:T(2,128)S(1)}, f32[1,2,1024]{2,1,0:T(2,128)S(1)}, u32[]{:S(2)}, u32[]{:S(2)}) collective-permute-start(f32[1,2,1024]{2,1,0:T(2,128)S(1)} %stack_reshape_squeeze.46), channel_id=1, source_target_pairs={{1,0},{2,1},{3,2},{4,3},{5,4},{6,5},{7,6},{8,7},{9,8},{10,9},{11,1... | collective-permute-start | bytes 24584 | tf_op jit(solution)/shard_map/ppermute | solution.py:23
  977.0 6.3 copy-start.15
  977.0 6.3 copy-start.17
  977.0 6.3 copy-start.19
  977.0 6.3 copy-start.50
  977.0 6.3 copy-start.53
  983.3 72.4 %copy-start.40 = (f32[1,1,2,32,1024]{4,3,2,1,0:T(8,128)S(1)}, f32[1,1,2,32,1024]{4,3,2,1,0:T(8,128)}, u32[]{:S(2)}) copy-start(f32[1,1,2,32,1024]{4,3,2,1,0:T(8,128)} %param.10) | copy-start | bytes 786436
  983.3 72.4 %copy-start.75 = (pred[32,1024]{1,0:T(8,128)(4,1)S(1)}, pred[32,1024]{1,0:T(8,128)(4,1)}, u32[]{:S(2)}) copy-start(pred[32,1024]{1,0:T(8,128)(4,1)} %copy-done.73) | copy-start | bytes 98308
  983.3 72.4 %copy-start.78 = (pred[32,1024]{1,0:T(8,128)(4,1)S(1)}, pred[32,1024]{1,0:T(8,128)(4,1)}, u32[]{:S(2)}) copy-start(pred[32,1024]{1,0:T(8,128)(4,1)} %copy-done.76) | copy-start | bytes 98308
  1055.7 6.0 copy-start.56
  (115 other events, 334.1 us)
where the time goes:
time: 1080 us; the launch traced here: 1060 us
  blocking collectives  546 us (51%)
  local copies, waits for them, and re-layouts  336 us (31%)
  other arithmetic  139 us (13%)
  starting transfers between devices  22.7 us (2%)
  between operations  15.9 us (1%)
    psum x5, blocking collectives, global_sum(): return lax.psum(jnp.sum(values), ('brick', 'grp'))  327 us
    another operation x3, blocking collectives, coarse_solve(): lax.linalg.triangular_solve(factor, gathered_terms, left_side=True, lower...  116 us
    all_gather x6, blocking collectives, apply_operator(): portion = lax.all_gather(outgoing_sides[None], 'brick', axis=0, tiled=True)  77.9 us
    broadcast_in_dim x26, local copies, waits for them, and re-layouts, apply_operator(): jnp.where(cube_third == BS - 1, from_above, jnp.roll(cube, -1, axis=3))  45 us
    broadcast_in_dim x26, local copies, waits for them, and re-layouts, apply_operator(): jnp.where(cube_third == 0, from_below, jnp.roll(cube, 1, axis=3))  43.7 us
    concatenate x12, local copies, waits for them, and re-layouts, apply_operator(): jnp.roll(cube, -1, axis=3)  26.6 us
    concatenate x12, local copies, waits for them, and re-layouts, apply_operator(): jnp.roll(cube, 1, axis=3)  25.4 us
    all_gather x1, blocking collectives, on_device(): gathered = lax.all_gather(record, 'grp', axis=0, tiled=True)  25.4 us
  transfers between devices with their start and end apart: 12, of which 0 were waited for; matrix products, arithmetic and copies ran while one was open for 21% of the time, Pallas kernels for 0%

commit v1 on v0

--- a/solution.py
+++ b/solution.py
@@ -185,44 +185,82 @@
     for direction in range(4):
         coarse_diag = coarse_diag + face_sums[direction] * inside[direction]
     coarse_diag = coarse_diag + face_sums[4] + face_sums[5]
+    grp_count = lax.axis_size("grp")
+    grp_ids = jnp.arange(grp_count, dtype=jnp.int32)
+
+    def butterfly(values, axes):
+        for axis in axes:
+            count = lax.axis_size(axis)
+            if count & (count - 1):
+                values = lax.psum(values, axis)
+                continue
+            stride = 1
+            while stride < count:
+                pairs = [(i, i ^ stride) for i in range(count)]
+                values = values + lax.ppermute(values, axis, pairs)
+                stride *= 2
+        return values
+
+    def slab_slot(values):
+        here = (grp_ids == slab_index).astype(jnp.float32)
+        return here[:, None, None] * values[None]
+
+    forcing = source[0, 0] * live_here
     record = jnp.stack(
-        [coarse_diag, face_sums[0] * inside[0], face_sums[2] * inside[2], face_sums[4]]
-    )[None]
-    gathered = lax.all_gather(record, "grp", axis=0, tiled=True)
-    columns = jnp.transpose(gathered, (1, 0, 2)).reshape(4, -1)
+        [
+            coarse_diag,
+            face_sums[0] * inside[0],
+            face_sums[2] * inside[2],
+            face_sums[4],
+            jnp.sum(forcing, axis=(1, 2)),
+        ]
+    )
+    gathered = butterfly(slab_slot(record), ("grp",))
+    columns = jnp.transpose(gathered, (1, 0, 2)).reshape(5, -1)
     matrix = assemble(columns[0], (columns[1], columns[2], columns[3]), (PATCH_Y, 1, slot_count))
     factor = jnp.linalg.cholesky(matrix)
 
-    def coarse_solve(residual_field):
-        totals = jnp.sum(residual_field, axis=(1, 2))
-        gathered_terms = lax.all_gather(totals[None], "grp", axis=0, tiled=True).reshape(-1, 1)
-        middle = lax.linalg.triangular_solve(factor, gathered_terms, left_side=True, lower=True)
+    def coarse_solve(terms):
+        middle = lax.linalg.triangular_solve(factor, terms[:, None], left_side=True, lower=True)
         result = lax.linalg.triangular_solve(
             factor, middle, left_side=True, lower=True, transpose_a=True
         )
         return lax.dynamic_slice_in_dim(result[:, 0], slab_index * slot_count, slot_count)
 
-    def precondition(residual_field):
+    def precondition(residual_field, terms):
         smoothed = OMEGA * residual_field / diagonal
         smoothed = smoothed + OMEGA * (residual_field - apply_operator(smoothed)) / diagonal
-        return smoothed + coarse_solve(residual_field)[:, None, None]
-
-    forcing = source[0, 0] * live_here
+        return smoothed + coarse_solve(terms)[:, None, None]
+
+    brick_here = (peer_ids == brick_index).astype(jnp.float32)
+
+    def dot_and_sums(product, field):
+        sums = slab_slot(jnp.sum(field, axis=(1, 2))[None])[:, 0]
+        spread = brick_here[:, None, None] * sums[None]
+        packed = jnp.concatenate([jnp.sum(product)[None], spread.reshape(-1)])
+        total = butterfly(packed, ("brick", "grp"))
+        mine = lax.dynamic_index_in_dim(
+            total[1:].reshape(brick_count, -1), brick_index, keepdims=False
+        )
+        return total[0], mine
+
+    def global_sum(values):
+        return butterfly(jnp.sum(values)[None], ("brick", "grp"))[0]
+
+    terms = columns[4]
     solution_field = jnp.zeros_like(forcing)
     residual = forcing
-
-    def global_sum(values):
-        return lax.psum(jnp.sum(values), ("brick", "grp"))
-
-    search = precondition(residual)
+    search = precondition(residual, terms)
     energy = global_sum(residual * search)
     for iteration in range(ITERS):
         mapped = apply_operator(search)
-        step_size = energy / global_sum(search * mapped)
+        curvature, mapped_terms = dot_and_sums(search * mapped, mapped)
+        step_size = energy / curvature
         solution_field = solution_field + step_size * search
         residual = residual - step_size * mapped
         if iteration + 1 < ITERS:
-            smoothed = precondition(residual)
+            terms = terms - step_size * mapped_terms
+            smoothed = precondition(residual, terms)
             renewed = global_sum(residual * smoothed)
             search = smoothed + renewed / energy * search
             energy = renewed

time: 1080 us -> 810 us (0.75)
  blocking collectives: 546 us -> 78.8 us
  starting transfers between devices: 22.7 us -> 145 us
  waiting for transfers between devices: 0.03 us -> 54 us
    psum x5 -> x0, blocking collectives: 327 us -> none  [global_sum(): return lax.psum(jnp.sum(values), ('brick', 'grp'))]
    ppermute x0 -> x46, starting transfers between devices: none -> 124 us  [butterfly(): values = values + lax.ppermute(values, axis, pairs)]
    another operation x3 -> x0, blocking collectives: 116 us -> none  [coarse_solve(): lax.linalg.triangular_solve(factor, gathered_terms, left_side=True, lower...]
    ppermute x0 -> x46, waiting for transfers between devices: none -> 54 us  [butterfly(): values = values + lax.ppermute(values, axis, pairs)]
    all_gather x1 -> x0, blocking collectives: 25.4 us -> none  [on_device(): gathered = lax.all_gather(record, 'grp', axis=0, tiled=True)]
  transfers between devices with their start and end apart: 12 -> 58, of which waited for: 0 -> 34; matrix products, arithmetic and copies ran while one was open for 21% -> 30% of each run, Pallas kernels for 0% -> 0%
where the time goes in v1:
time: 810 us; the launch traced here: 796 us
  local copies, waits for them, and re-layouts  344 us (42%)
  other arithmetic  145 us (18%)
  starting transfers between devices  145 us (18%)
  blocking collectives  78.8 us (10%)
  waiting for transfers between devices  54 us (7%)
  between operations  25.7 us (3%)
    ppermute x46, starting transfers between devices, butterfly(): values = values + lax.ppermute(values, axis, pairs)  124 us
    all_gather x6, blocking collectives, apply_operator(): portion = lax.all_gather(outgoing_sides[None], 'brick', axis=0, tiled=True)  78.8 us
    ppermute x46, waiting for transfers between devices, butterfly(): values = values + lax.ppermute(values, axis, pairs)  54 us
    broadcast_in_dim x26, local copies, waits for them, and re-layouts, apply_operator(): jnp.where(cube_third == BS - 1, from_above, jnp.roll(cube, -1, axis=3))  46.7 us
    broadcast_in_dim x26, local copies, waits for them, and re-layouts, apply_operator(): jnp.where(cube_third == 0, from_below, jnp.roll(cube, 1, axis=3))  42.9 us
    concatenate x12, local copies, waits for them, and re-layouts, apply_operator(): jnp.roll(cube, 1, axis=3)  25.5 us
    concatenate x12, local copies, waits for them, and re-layouts, apply_operator(): jnp.roll(cube, -1, axis=3)  23 us
    concatenate x15, local copies, waits for them, and re-layouts, apply_operator(): jnp.concatenate([field[:, :, BS:], beyond_yplus], axis=2)  21.9 us
  transfers between devices with their start and end apart: 58, of which 34 were waited for; matrix products, arithmetic and copies ran while one was open for 30% of the time, Pallas kernels for 0%

profile of v1, /device:TPU:0, one launch (start us, length us, event | category | flops | bytes accessed | tf_op | source)
XLA Modules:
  0.0 795.7 jit_solution(16637626487733563843)
XLA Ops:
  31.3 5.5 multiply_divide_fusion.2
  46.3 2.5 collective-permute-start.1
  62.5 13.4 %all-gather = f32[32,2,1024]{2,1,0:T(2,128)S(1)} all-gather(f32[4,2,1024]{2,1,0:T(2,128)S(1)} %copy.421), channel_id=2, replica_groups=mesh['brick'=8,'grp'=16] {'brick'}, dimensions={0}, use_global_device_ids=true | all-gather | bytes 294912 | tf_op jit(solution)/shard_map/all_gather | solution.py:124
  84.2 5.6 collective-permute-start.3
  92.7 3.5 collective-permute-start.4
  102.1 3.0 collective-permute-start.5
  112.6 2.9 cholesky.19
  121.3 8.5 %fusion.46 = (f32[2,32,32,32]{3,2,1,0:T(8,128)S(1)}, f32[2,32,32,32]{3,2,1,0:T(8,128)}, f32[2,32,32,32]{3,2,1,0:T(8,128)}) fusion(f32[2,32,32,32]{3,2,1,0:T(8,128)} %get-tuple-element.73, f32[2,32,32,32]{3,2,1,0:T(8,128)} %copy-done.15, f32[2,32,32,32]{3,2,1,0:T(8,128)} %copy-done.14, f32[2,32,32,32]{3,2,1,0:T(8,128)} %concatenate.668, ...), kind=kLoop, calls=%fused_computation.88 | loop fusion | flops 2293760 | bytes 4538480 | tf_op jit(solution)/shard_map/add | solution.py:233
  152.9 12.8 %all-gather.1 = f32[32,2,1024]{2,1,0:T(2,128)S(1)} all-gather(f32[4,2,1024]{2,1,0:T(2,128)S(1)} %copy.424), channel_id=3, replica_groups=mesh['brick'=8,'grp'=16] {'brick'}, dimensions={0}, use_global_device_ids=true | all-gather | bytes 294912 | tf_op jit(solution)/shard_map/all_gather | solution.py:124
  181.4 3.0 pad_maximum_fusion.2
  206.9 3.8 multiply_reduce_fusion.4
  222.3 3.2 collective-permute-done.17
  225.5 2.6 collective-permute-start.18
  229.7 3.5 collective-permute-start.19
  235.4 4.4 collective-permute-start.20
  254.8 2.7 collective-permute-start.7
  259.0 3.3 collective-permute-start.8
  270.3 3.7 collective-permute-done.10
  278.8 3.7 collective-permute-start.12
  296.8 13.2 %all-gather.2 = f32[32,2,1024]{2,1,0:T(2,128)S(1)} all-gather(f32[4,2,1024]{2,1,0:T(2,128)S(1)} %copy.430), channel_id=4, replica_groups=mesh['brick'=8,'grp'=16] {'brick'}, dimensions={0}, use_global_device_ids=true | all-gather | bytes 294912 | tf_op jit(solution)/shard_map/all_gather | solution.py:124
  315.7 6.9 multiply_divide_fusion.1
  332.4 2.5 collective-permute-start.23
  338.7 3.0 pad_maximum_fusion.4
  372.2 3.8 multiply_reduce_fusion.3
  381.9 2.7 collective-permute-start.25
  386.1 3.3 collective-permute-start.26
  391.8 4.0 collective-permute-start.27
  396.5 3.8 collective-permute-start.28
  402.3 5.7 collective-permute-start.29
  408.8 4.9 collective-permute-start.30
  417.2 13.0 %all-gather.3 = f32[32,2,1024]{2,1,0:T(2,128)S(1)} all-gather(f32[4,2,1024]{2,1,0:T(2,128)S(1)} %copy.435), channel_id=5, replica_groups=mesh['brick'=8,'grp'=16] {'brick'}, dimensions={0}, use_global_device_ids=true | all-gather | bytes 294912 | tf_op jit(solution)/shard_map/all_gather | solution.py:124
  434.1 6.3 multiply_add_fusion.1
  447.6 2.7 pad_maximum_fusion.6
  467.3 3.4 multiply_reduce_fusion.2
  479.1 3.2 collective-permute-done.35
  482.3 2.6 collective-permute-start.36
  486.5 4.1 collective-permute-start.37
  492.2 5.5 collective-permute-start.38
  499.9 3.6 collective-permute-start.39
  517.4 13.1 %all-gather.4 = f32[32,2,1024]{2,1,0:T(2,128)S(1)} all-gather(f32[4,2,1024]{2,1,0:T(2,128)S(1)} %copy.440), channel_id=6, replica_groups=mesh['brick'=8,'grp'=16] {'brick'}, dimensions={0}, use_global_device_ids=true | all-gather | bytes 294912 | tf_op jit(solution)/shard_map/all_gather | solution.py:124
  535.4 6.6 multiply_divide_fusion
  556.8 3.1 pad_maximum_fusion.8
  589.0 3.9 multiply_reduce_fusion.1
  598.7 2.6 collective-permute-start.43
  603.1 3.3 collective-permute-start.44
  608.9 4.0 collective-permute-start.45
  613.9 3.0 collective-permute-start.46
  619.7 4.9 collective-permute-start.47
  625.6 4.0 collective-permute-start.48
  641.0 13.2 %all-gather.5 = f32[32,2,1024]{2,1,0:T(2,128)S(1)} all-gather(f32[4,2,1024]{2,1,0:T(2,128)S(1)} %copy.445), channel_id=7, replica_groups=mesh['brick'=8,'grp'=16] {'brick'}, dimensions={0}, use_global_device_ids=true | all-gather | bytes 294912 | tf_op jit(solution)/shard_map/all_gather | solution.py:124
  659.3 9.3 %multiply_add_fusion = f32[2,32,32,32]{3,2,1,0:T(8,128)S(1)} fusion(f32[2,32,32,32]{3,2,1,0:T(8,128)} %copy-done.16, f32[2,32,32,32]{3,2,1,0:T(8,128)} %get-tuple-element.73, f32[2,32,32,32]{3,2,1,0:T(8,128)} %copy-done.15, f32[2,32,32,32]{3,2,1,0:T(8,128)} %copy-done.14, f32[2,32,32,32]{3,2,1,0:T(8,128)} %concatenate.784, ...), kind=kLoop, calls=%fused_computation.76 | loop fusion | flops 3735552 | bytes 5865592 | tf_op jit(solution)/shard_map/add | solution.py:265
  686.7 2.6 broadcast_in_dim.796
  706.1 3.2 collective-permute-done.53
  709.3 2.6 collective-permute-start.54
  713.5 3.8 collective-permute-start.55
  723.7 2.5 broadcast_in_dim.759
  731.3 2.5 concatenate.738
  740.0 3.9 fusion.96
  751.7 2.8 collective-permute-start.57
  764.3 2.5 broadcast_in_dim.799
  771.9 2.5 concatenate.817
  775.6 2.5 broadcast_in_dim.800
  783.1 2.5 broadcast_in_dim.803
  788.8 5.9 fusion.148
  (938 shorter events, 469.3 us)
Async XLA Ops:
  5.1 100.0 %copy-start.121 = (pred[32]{0:T(512)(128)(4,1)}, pred[32]{0:T(512)(128)(4,1)S(1)}, u32[]{:S(2)}) copy-start(pred[32]{0:T(512)(128)(4,1)S(1)} %get-tuple-element.280) | copy-start | bytes 100
  5.1 100.6 %copy-start.127 = (pred[32]{0:T(512)(128)(4,1)}, pred[32]{0:T(512)(128)(4,1)S(1)}, u32[]{:S(2)}) copy-start(pred[32]{0:T(512)(128)(4,1)S(1)} %get-tuple-element.281) | copy-start | bytes 100
  15.0 357.2 %copy-start.21 = (f32[2,32,1024]{2,1,0:T(8,128)}, f32[2,32,1024]{2,1,0:T(8,128)S(1)}, u32[]{:S(2)}) copy-start(f32[2,32,1024]{2,1,0:T(8,128)S(1)} %get-tuple-element.70) | copy-start | bytes 786436
  40.5 42.8 %collective-permute-start.2 = (f32[16,5,2]{2,0,1:T(8,128)}, f32[16,5,2]{2,0,1:T(8,128)}, u32[]{:S(2)}, u32[]{:S(2)}) collective-permute-start(f32[16,5,2]{2,0,1:T(8,128)} %broadcast_multiply_fusion.3), channel_id=1, source_target_pairs={{0,1},{1,0},{2,3},{3,2},{4,5},{5,4},{6,7},{7,6},{8,9},{9,8},{10,11... | collective-permute-start | bytes 1928 | tf_op jit(solution)/shard_map/ppermute | solution.py:200
  46.3 74.2 %collective-permute-start.1 = (f32[1,2,1024]{2,1,0:T(2,128)}, f32[1,2,1024]{2,1,0:T(2,128)}, u32[]{:S(2)}, u32[]{:S(2)}) collective-permute-start(f32[1,2,1024]{2,1,0:T(2,128)} %stack_reshape_squeeze.37), channel_id=1, source_target_pairs={{0,1},{1,2},{2,3},{3,4},{4,5},{5,6},{6,7},{7,8},{8,9},{9,10},{10,1... | collective-permute-start | bytes 24584 | tf_op jit(solution)/shard_map/ppermute | solution.py:20
  50.3 69.5 %collective-permute-start = (f32[1,2,1024]{2,1,0:T(2,128)}, f32[1,2,1024]{2,1,0:T(2,128)}, u32[]{:S(2)}, u32[]{:S(2)}) collective-permute-start(f32[1,2,1024]{2,1,0:T(2,128)} %stack_reshape_squeeze.36), channel_id=1, source_target_pairs={{1,0},{2,1},{3,2},{4,3},{5,4},{6,5},{7,6},{8,7},{9,8},{10,9},{11,1... | collective-permute-start | bytes 24584 | tf_op jit(solution)/shard_map/ppermute | solution.py:23
  84.2 7.6 collective-permute-start.3
  92.7 9.4 %collective-permute-start.4 = (f32[16,5,2]{2,0,1:T(8,128)S(1)}, f32[16,5,2]{2,0,1:T(8,128)S(1)}, u32[]{:S(2)}, u32[]{:S(2)}) collective-permute-start(f32[16,5,2]{2,0,1:T(8,128)S(1)} %fusion.258), channel_id=1, source_target_pairs={{0,4},{1,5},{2,6},{3,7},{4,0},{5,1},{6,2},{7,3},{8,12},{9,13},{10,... | collective-permute-start | bytes 1928 | tf_op jit(solution)/shard_map/ppermute | solution.py:200
  102.1 9.6 %collective-permute-start.5 = (f32[16,5,2]{2,0,1:T(8,128)S(1)}, f32[16,5,2]{2,0,1:T(8,128)S(1)}, u32[]{:S(2)}, u32[]{:S(2)}) collective-permute-start(f32[16,5,2]{2,0,1:T(8,128)S(1)} %add.671), channel_id=1, source_target_pairs={{0,8},{1,9},{2,10},{3,11},{4,12},{5,13},{6,14},{7,15},{8,0},{9,1},... | collective-permute-start | bytes 1928 | tf_op jit(solution)/shard_map/ppermute | solution.py:200
  176.7 18.5 %collective-permute-start.14 = (f32[1,2,1024]{2,1,0:T(2,128)}, f32[1,2,1024]{2,1,0:T(2,128)}, u32[]{:S(2)}, u32[]{:S(2)}) collective-permute-start(f32[1,2,1024]{2,1,0:T(2,128)} %stack_reshape_squeeze.39), channel_id=1, source_target_pairs={{0,1},{1,2},{2,3},{3,4},{4,5},{5,6},{6,7},{7,8},{8,9},{9,10},{10,1... | collective-permute-start | bytes 24584 | tf_op jit(solution)/shard_map/ppermute | solution.py:20
  178.6 22.5 %collective-permute-start.13 = (f32[1,2,1024]{2,1,0:T(2,128)}, f32[1,2,1024]{2,1,0:T(2,128)}, u32[]{:S(2)}, u32[]{:S(2)}) collective-permute-start(f32[1,2,1024]{2,1,0:T(2,128)} %stack_reshape_squeeze.38), channel_id=1, source_target_pairs={{1,0},{2,1},{3,2},{4,3},{5,4},{6,5},{7,6},{8,7},{9,8},{10,9},{11,1... | collective-permute-start | bytes 24584 | tf_op jit(solution)/shard_map/ppermute | solution.py:23
  214.3 1.2 collective-permute-start.15
  216.8 3.6 collective-permute-start.16
  220.4 5.1 collective-permute-start.17
  225.5 4.2 collective-permute-start.18
  229.7 5.1 collective-permute-start.19
  235.4 16.3 %collective-permute-start.20 = (f32[257]{0:T(512)}, f32[257]{0:T(512)}, u32[]{:S(2)}, u32[]{:S(2)}) collective-permute-start(f32[257]{0:T(512)} %add.700), channel_id=1, source_target_pairs={{0,4},{1,5},{2,6},{3,7},{4,0},{5,1},{6,2},{7,3},{8,12},{9,13},{10,... | collective-permute-start | bytes 3092 | tf_op jit(solution)/shard_map/ppermute | solution.py:200
  247.0 6.6 collective-permute-start.6
  252.4 32.1 %collective-permute-start.21 = (f32[257]{0:T(512)S(1)}, f32[257]{0:T(512)S(1)}, u32[]{:S(2)}, u32[]{:S(2)}) collective-permute-start(f32[257]{0:T(512)S(1)} %add.701), channel_id=1, source_target_pairs={{0,8},{1,9},{2,10},{3,11},{4,12},{5,13},{6,14},{7,15},{8,0},{9,1},... | collective-permute-start | bytes 3092 | tf_op jit(solution)/shard_map/ppermute | solution.py:200
  254.8 3.6 collective-permute-start.7
  259.0 5.1 collective-permute-start.8
  264.7 3.6 collective-permute-start.9
  268.9 5.1 collective-permute-start.10
  274.6 3.6 collective-permute-start.11
  278.8 5.1 collective-permute-start.12
  332.4 28.0 %collective-permute-start.23 = (f32[1,2,1024]{2,1,0:T(2,128)}, f32[1,2,1024]{2,1,0:T(2,128)}, u32[]{:S(2)}, u32[]{:S(2)}) collective-permute-start(f32[1,2,1024]{2,1,0:T(2,128)} %stack_reshape_squeeze.41), channel_id=1, source_target_pairs={{0,1},{1,2},{2,3},{3,4},{4,5},{5,6},{6,7},{7,8},{8,9},{9,10},{10,1... | collective-permute-start | bytes 24584 | tf_op jit(solution)/shard_map/ppermute | solution.py:20
  334.9 31.4 %collective-permute-start.22 = (f32[1,2,1024]{2,1,0:T(2,128)}, f32[1,2,1024]{2,1,0:T(2,128)}, u32[]{:S(2)}, u32[]{:S(2)}) collective-permute-start(f32[1,2,1024]{2,1,0:T(2,128)} %stack_reshape_squeeze.40), channel_id=1, source_target_pairs={{1,0},{2,1},{3,2},{4,3},{5,4},{6,5},{7,6},{8,7},{9,8},{10,9},{11,1... | collective-permute-start | bytes 24584 | tf_op jit(solution)/shard_map/ppermute | solution.py:23
  375.9 4.7 collective-permute-start.24
  381.9 3.6 collective-permute-start.25
  386.1 5.1 collective-permute-start.26
  391.8 4.1 collective-permute-start.27
  396.5 5.1 collective-permute-start.28
  402.3 5.9 collective-permute-start.29
  408.8 5.1 collective-permute-start.30
  444.3 13.6 %collective-permute-start.32 = (f32[1,2,1024]{2,1,0:T(2,128)S(1)}, f32[1,2,1024]{2,1,0:T(2,128)S(1)}, u32[]{:S(2)}, u32[]{:S(2)}) collective-permute-start(f32[1,2,1024]{2,1,0:T(2,128)S(1)} %stack_reshape_squeeze.43), channel_id=1, source_target_pairs={{0,1},{1,2},{2,3},{3,4},{4,5},{5,6},{6,7},{7,8},{8,9},{9,10},{10,1... | collective-permute-start | bytes 24584 | tf_op jit(solution)/shard_map/ppermute | solution.py:20
  446.3 16.3 %collective-permute-start.31 = (f32[1,2,1024]{2,1,0:T(2,128)}, f32[1,2,1024]{2,1,0:T(2,128)}, u32[]{:S(2)}, u32[]{:S(2)}) collective-permute-start(f32[1,2,1024]{2,1,0:T(2,128)} %stack_reshape_squeeze.42), channel_id=1, source_target_pairs={{1,0},{2,1},{3,2},{4,3},{5,4},{6,5},{7,6},{8,7},{9,8},{10,9},{11,1... | collective-permute-start | bytes 24584 | tf_op jit(solution)/shard_map/ppermute | solution.py:23
  470.7 37.8 %copy-start.76 = (f32[2,31,1024]{2,1,0:T(8,128)S(1)}, f32[2,31,1024]{2,1,0:T(8,128)}, u32[]{:S(2)}) copy-start(f32[2,31,1024]{2,1,0:T(8,128)} %get-tuple-element.133) | copy-start | bytes 761860
  470.7 39.1 %copy-start.82 = (f32[2,32,1024]{2,1,0:T(8,128)S(1)}, f32[2,32,1024]{2,1,0:T(8,128)}, u32[]{:S(2)}) copy-start(f32[2,32,1024]{2,1,0:T(8,128)} %get-tuple-element.50) | copy-start | bytes 786436
  471.7 1.2 collective-permute-start.33
  473.6 3.6 collective-permute-start.34
  477.2 5.1 collective-permute-start.35
  482.3 4.2 collective-permute-start.36
  486.5 5.7 collective-permute-start.37
  492.2 7.1 collective-permute-start.38
  499.9 12.6 %collective-permute-start.39 = (f32[257]{0:T(512)}, f32[257]{0:T(512)}, u32[]{:S(2)}, u32[]{:S(2)}) collective-permute-start(f32[257]{0:T(512)} %add.733), channel_id=1, source_target_pairs={{0,8},{1,9},{2,10},{3,11},{4,12},{5,13},{6,14},{7,15},{8,0},{9,1},... | collective-permute-start | bytes 3092 | tf_op jit(solution)/shard_map/ppermute | solution.py:200
  551.6 25.7 %collective-permute-start.41 = (f32[1,2,1024]{2,1,0:T(2,128)}, f32[1,2,1024]{2,1,0:T(2,128)}, u32[]{:S(2)}, u32[]{:S(2)}) collective-permute-start(f32[1,2,1024]{2,1,0:T(2,128)} %stack_reshape_squeeze.45), channel_id=1, source_target_pairs={{0,1},{1,2},{2,3},{3,4},{4,5},{5,6},{6,7},{7,8},{8,9},{9,10},{10,1... | collective-permute-start | bytes 24584 | tf_op jit(solution)/shard_map/ppermute | solution.py:20
  554.1 29.1 %collective-permute-start.40 = (f32[1,2,1024]{2,1,0:T(2,128)}, f32[1,2,1024]{2,1,0:T(2,128)}, u32[]{:S(2)}, u32[]{:S(2)}) collective-permute-start(f32[1,2,1024]{2,1,0:T(2,128)} %stack_reshape_squeeze.44), channel_id=1, source_target_pairs={{1,0},{2,1},{3,2},{4,3},{5,4},{6,5},{7,6},{8,7},{9,8},{10,9},{11,1... | collective-permute-start | bytes 24584 | tf_op jit(solution)/shard_map/ppermute | solution.py:23
  592.9 4.6 collective-permute-start.42
  595.3 59.0 %copy-start.191 = (pred[8,4]{1,0:T(8,128)(4,1)S(1)}, pred[8,4]{1,0:T(8,128)(4,1)}, u32[]{:S(2)}) copy-start(pred[8,4]{1,0:T(8,128)(4,1)} %copy-done.189) | copy-start | bytes 100
  598.7 3.7 collective-permute-start.43
  603.1 5.2 collective-permute-start.44
  608.9 4.3 collective-permute-start.45
  613.9 5.2 collective-permute-start.46
  619.7 5.3 collective-permute-start.47
  625.6 5.2 collective-permute-start.48
  672.8 12.3 %collective-permute-start.50 = (f32[1,2,1024]{2,1,0:T(2,128)S(1)}, f32[1,2,1024]{2,1,0:T(2,128)S(1)}, u32[]{:S(2)}, u32[]{:S(2)}) collective-permute-start(f32[1,2,1024]{2,1,0:T(2,128)S(1)} %stack_reshape_squeeze.47), channel_id=1, source_target_pairs={{0,1},{1,2},{2,3},{3,4},{4,5},{5,6},{6,7},{7,8},{8,9},{9,10},{10,1... | collective-permute-start | bytes 24584 | tf_op jit(solution)/shard_map/ppermute | solution.py:20
  675.2 14.0 %collective-permute-start.49 = (f32[1,2,1024]{2,1,0:T(2,128)}, f32[1,2,1024]{2,1,0:T(2,128)}, u32[]{:S(2)}, u32[]{:S(2)}) collective-permute-start(f32[1,2,1024]{2,1,0:T(2,128)} %stack_reshape_squeeze.46), channel_id=1, source_target_pairs={{1,0},{2,1},{3,2},{4,3},{5,4},{6,5},{7,6},{8,7},{9,8},{10,9},{11,1... | collective-permute-start | bytes 24584 | tf_op jit(solution)/shard_map/ppermute | solution.py:23
  698.7 1.2 collective-permute-start.51
  700.6 3.6 collective-permute-start.52
  704.2 5.1 collective-permute-start.53
  709.3 4.2 collective-permute-start.54
  713.5 23.9 %collective-permute-start.55 = (f32[257]{0:T(512)S(1)}, f32[257]{0:T(512)S(1)}, u32[]{:S(2)}, u32[]{:S(2)}) collective-permute-start(f32[257]{0:T(512)S(1)} %add.759), channel_id=1, source_target_pairs={{0,2},{1,3},{2,0},{3,1},{4,6},{5,7},{6,4},{7,5},{8,10},{9,11},{10,... | collective-permute-start | bytes 3092 | tf_op jit(solution)/shard_map/ppermute | solution.py:200
  738.0 12.3 %collective-permute-start.56 = (f32[257]{0:T(512)}, f32[257]{0:T(512)}, u32[]{:S(2)}, u32[]{:S(2)}) collective-permute-start(f32[257]{0:T(512)} %add.760), channel_id=1, source_target_pairs={{0,4},{1,5},{2,6},{3,7},{4,0},{5,1},{6,2},{7,3},{8,12},{9,13},{10,... | collective-permute-start | bytes 3092 | tf_op jit(solution)/shard_map/ppermute | solution.py:200
  751.7 35.1 %collective-permute-start.57 = (f32[257]{0:T(512)}, f32[257]{0:T(512)}, u32[]{:S(2)}, u32[]{:S(2)}) collective-permute-start(f32[257]{0:T(512)} %add.761), channel_id=1, source_target_pairs={{0,8},{1,9},{2,10},{3,11},{4,12},{5,13},{6,14},{7,15},{8,0},{9,1},... | collective-permute-start | bytes 3092 | tf_op jit(solution)/shard_map/ppermute | solution.py:200
  (221 other events, 1256.4 us)

commit v2 on v1

--- a/solution.py
+++ b/solution.py
@@ -1,7 +1,13 @@
+import functools
+
 import jax
 import jax.numpy as jnp
 from jax import lax
+from jax.experimental import pallas as pl
+from jax.experimental.pallas import tpu as pltpu
 from jax.sharding import PartitionSpec as P
+
+MESH_IDS = pl.DeviceIdType.MESH
 
 BS = 32
 PATCH_X = 1
@@ -10,6 +16,68 @@
 
 
 OMEGA = 0.6
+
+
+def allsum2_kernel(x_ref, o_ref, landed_b, landed_g, send_b, recv_b, send_g, recv_g):
+    here_brick = lax.axis_index("brick")
+    here_grp = lax.axis_index("grp")
+    n_brick = landed_b.shape[0]
+    n_grp = landed_g.shape[0]
+    brick_peers = [(lax.rem(here_brick + k, n_brick), here_grp) for k in range(1, n_brick)]
+    grp_peers = [(here_brick, lax.rem(here_grp + k, n_grp)) for k in range(1, n_grp)]
+    barrier = pltpu.get_barrier_semaphore()
+    for peer in brick_peers + grp_peers:
+        pl.semaphore_signal(barrier, inc=1, device_id=peer, device_id_type=MESH_IDS)
+    pl.semaphore_wait(barrier, len(brick_peers) + len(grp_peers))
+
+    def exchange(src, landed, sends, recvs, peers):
+        copies = []
+        for k, peer in enumerate(peers, start=1):
+            copy = pltpu.make_async_remote_copy(
+                src_ref=src,
+                dst_ref=landed.at[k],
+                send_sem=sends.at[k],
+                recv_sem=recvs.at[k],
+                device_id=peer,
+                device_id_type=MESH_IDS,
+            )
+            copy.start()
+            copies.append(copy)
+        for copy in copies:
+            copy.wait()
+
+    landed_b[0] = x_ref[...]
+    exchange(x_ref, landed_b, send_b, recv_b, brick_peers)
+    total = landed_b[lax.rem(here_brick, n_brick)]
+    for j in range(1, n_brick):
+        total = total + landed_b[lax.rem(here_brick + n_brick - j, n_brick)]
+    o_ref[...] = total
+    landed_g[0] = total
+    exchange(o_ref, landed_g, send_g, recv_g, grp_peers)
+    total = landed_g[lax.rem(here_grp, n_grp)]
+    for j in range(1, n_grp):
+        total = total + landed_g[lax.rem(here_grp + n_grp - j, n_grp)]
+    o_ref[...] = total
+
+
+def allsum2_tile(tile, kernel_id):
+    n_brick = lax.axis_size("brick")
+    n_grp = lax.axis_size("grp")
+    return pl.pallas_call(
+        allsum2_kernel,
+        out_shape=jax.ShapeDtypeStruct(tile.shape, jnp.float32),
+        in_specs=[pl.BlockSpec(memory_space=pltpu.VMEM)],
+        out_specs=pl.BlockSpec(memory_space=pltpu.VMEM),
+        scratch_shapes=[
+            pltpu.VMEM((n_brick,) + tile.shape, jnp.float32),
+            pltpu.VMEM((n_grp,) + tile.shape, jnp.float32),
+            pltpu.SemaphoreType.DMA((n_brick,)),
+            pltpu.SemaphoreType.DMA((n_brick,)),
+            pltpu.SemaphoreType.DMA((n_grp,)),
+            pltpu.SemaphoreType.DMA((n_grp,)),
+        ],
+        compiler_params=pltpu.CompilerParams(collective_id=kernel_id, has_side_effects=True),
+    )(tile)
 
 
 def extended_2(block, sides, width):
@@ -215,7 +283,15 @@
             jnp.sum(forcing, axis=(1, 2)),
         ]
     )
-    gathered = butterfly(slab_slot(record), ("grp",))
+    brick_here = (peer_ids == brick_index).astype(jnp.float32)
+    spread = (brick_here[:, None, None, None] * slab_slot(record)[None]).reshape(-1)
+    rows = -(-spread.shape[0] // 128)
+    rows = -(-rows // 8) * 8
+    tile = jnp.pad(spread, (0, rows * 128 - spread.shape[0])).reshape(rows, 128)
+    summed = allsum2_tile(tile, 2).reshape(-1)[: spread.shape[0]]
+    gathered = lax.dynamic_index_in_dim(
+        summed.reshape(brick_count, grp_count, 5, slot_count), brick_index, keepdims=False
+    )
     columns = jnp.transpose(gathered, (1, 0, 2)).reshape(5, -1)
     matrix = assemble(columns[0], (columns[1], columns[2], columns[3]), (PATCH_Y, 1, slot_count))
     factor = jnp.linalg.cholesky(matrix)
@@ -232,20 +308,24 @@
         smoothed = smoothed + OMEGA * (residual_field - apply_operator(smoothed)) / diagonal
         return smoothed + coarse_solve(terms)[:, None, None]
 
-    brick_here = (peer_ids == brick_index).astype(jnp.float32)
+    def allsum(values):
+        rows = -(-values.shape[0] // 128)
+        rows = -(-rows // 8) * 8
+        tile = jnp.pad(values, (0, rows * 128 - values.shape[0])).reshape(rows, 128)
+        return allsum2_tile(tile, 1).reshape(-1)[: values.shape[0]]
 
     def dot_and_sums(product, field):
         sums = slab_slot(jnp.sum(field, axis=(1, 2))[None])[:, 0]
         spread = brick_here[:, None, None] * sums[None]
         packed = jnp.concatenate([jnp.sum(product)[None], spread.reshape(-1)])
-        total = butterfly(packed, ("brick", "grp"))
+        total = allsum(packed)
         mine = lax.dynamic_index_in_dim(
             total[1:].reshape(brick_count, -1), brick_index, keepdims=False
         )
         return total[0], mine
 
     def global_sum(values):
-        return butterfly(jnp.sum(values)[None], ("brick", "grp"))[0]
+        return allsum(jnp.sum(values)[None])[0]
 
     terms = columns[4]
     solution_field = jnp.zeros_like(forcing)

time: 810 us -> 746 us (0.921)
  starting transfers between devices: 145 us -> 27.7 us
  Pallas kernels: 0 us -> 112 us
  waiting for transfers between devices: 54 us -> 0.03 us
  local copies, waits for them, and re-layouts: 344 us -> 355 us
  between operations: 25.7 us -> 14.7 us
    ppermute x46 -> x0, starting transfers between devices: 124 us -> none  [butterfly(): values = values + lax.ppermute(values, axis, pairs)]
    pallas_call x0 -> x7, Pallas kernels: none -> 112 us  [allsum2_tile(): pl.pallas_call(allsum2_kernel, out_shape=jax.ShapeDtypeStruct(tile.shape,...]
    ppermute x46 -> x0, waiting for transfers between devices: 54 us -> none  [butterfly(): values = values + lax.ppermute(values, axis, pairs)]
    add x24 -> x0, other arithmetic: 9.76 us -> none  [butterfly(): values = values + lax.ppermute(values, axis, pairs)]
  transfers between devices with their start and end apart: 58 -> 12, of which waited for: 34 -> 0; matrix products, arithmetic and copies ran while one was open for 30% -> 31% of each run, Pallas kernels for 0% -> 2%
where the time goes in v2:
time: 746 us; the launch traced here: 734 us
  local copies, waits for them, and re-layouts  355 us (48%)
  other arithmetic  143 us (19%)
  Pallas kernels  112 us (15%)
  blocking collectives  78.6 us (11%)
  starting transfers between devices  27.7 us (4%)
  between operations  14.7 us (2%)
    pallas_call x7, Pallas kernels, allsum2_tile(): pl.pallas_call(allsum2_kernel, out_shape=jax.ShapeDtypeStruct(tile.shape,...  112 us
    all_gather x6, blocking collectives, apply_operator(): portion = lax.all_gather(outgoing_sides[None], 'brick', axis=0, tiled=True)  78.6 us
    broadcast_in_dim x26, local copies, waits for them, and re-layouts, apply_operator(): jnp.where(cube_third == BS - 1, from_above, jnp.roll(cube, -1, axis=3))  46 us
    broadcast_in_dim x26, local copies, waits for them, and re-layouts, apply_operator(): jnp.where(cube_third == 0, from_below, jnp.roll(cube, 1, axis=3))  42.5 us
    div x6, other arithmetic, precondition(): smoothed = OMEGA * residual_field / diagonal  26.7 us
    concatenate x12, local copies, waits for them, and re-layouts, apply_operator(): jnp.roll(cube, -1, axis=3)  26.5 us
    concatenate x12, local copies, waits for them, and re-layouts, apply_operator(): jnp.roll(cube, 1, axis=3)  25.5 us
    concatenate x15, local copies, waits for them, and re-layouts, apply_operator(): jnp.concatenate([field[:, :, BS:], beyond_yplus], axis=2)  21.7 us
  transfers between devices with their start and end apart: 12, of which 0 were waited for; matrix products, arithmetic and copies ran while one was open for 31% of the time, Pallas kernels for 2%

profile of v2, /device:TPU:0, one launch (start us, length us, event | category | flops | bytes accessed | tf_op | source)
XLA Modules:
  0.0 733.9 jit_solution(1511894146735439728)
XLA Ops:
  15.3 2.5 squeeze.134
  22.2 5.7 multiply_divide_fusion.2
  30.5 4.5 collective-permute-start.1
  47.7 13.5 %all-gather = f32[32,2,1024]{2,1,0:T(2,128)S(1)} all-gather(f32[4,2,1024]{2,1,0:T(2,128)S(1)} %copy.458), channel_id=2, replica_groups=mesh['brick'=8,'grp'=16] {'brick'}, dimensions={0}, use_global_device_ids=true | all-gather | bytes 294912 | tf_op jit(solution)/shard_map/all_gather | solution.py:192
  68.9 17.3 %shard_map.68 = f32[16,128]{1,0:T(8,128)} custom-call(f32[16,128]{1,0:T(8,128)} %pad_bitcast_fusion.x_ref), custom_call_target="tpu_custom_call" | custom-call | tf_op jit(solution)/shard_map/pallas_call | solution.py:66
  98.0 2.9 cholesky.19
  102.3 2.4 custom-call.14
  120.2 8.4 %fusion.46 = (f32[2,32,32,32]{3,2,1,0:T(8,128)S(1)}, f32[2,32,32,32]{3,2,1,0:T(8,128)}, f32[2,32,32,32]{3,2,1,0:T(8,128)}) fusion(f32[2,32,32,32]{3,2,1,0:T(8,128)} %get-tuple-element.73, f32[2,32,32,32]{3,2,1,0:T(8,128)} %get-tuple-element.75, f32[2,32,32,32]{3,2,1,0:T(8,128)} %get-tuple-element.74, f32[2,32,32,32]{3,2,1,0:T(8,128)} %concatenate.668, ...), kind=kLoop, calls=%fused_computation.88 | loop fusion | flops 2293760 | bytes 4538480 | tf_op jit(solution)/shard_map/add | solution.py:309
  128.6 2.4 concatenate.652
  131.0 2.4 concatenate.654
  134.8 2.4 broadcast_in_dim.714
  151.8 13.1 %all-gather.1 = f32[32,2,1024]{2,1,0:T(2,128)S(1)} all-gather(f32[4,2,1024]{2,1,0:T(2,128)S(1)} %copy.467), channel_id=3, replica_groups=mesh['brick'=8,'grp'=16] {'brick'}, dimensions={0}, use_global_device_ids=true | all-gather | bytes 294912 | tf_op jit(solution)/shard_map/all_gather | solution.py:192
  175.9 3.1 collective-permute-start.3
  181.6 3.0 pad_maximum_fusion.2
  189.0 2.4 concatenate.687
  191.4 2.4 broadcast_in_dim.761
  193.9 2.4 broadcast_in_dim.763
  207.3 2.4 concatenate.737
  212.1 2.4 concatenate.738
  214.5 2.5 concatenate.672
  233.4 2.4 broadcast_in_dim.780
  235.8 2.4 broadcast_in_dim.743
  238.2 3.8 multiply_reduce_fusion.4
  246.3 15.7 %shard_map.70 = f32[8,128]{1,0:T(8,128)} custom-call(f32[8,128]{1,0:T(8,128)} %fusion.180.x_ref), custom_call_target="tpu_custom_call" | custom-call | tf_op jit(solution)/shard_map/pallas_call | solution.py:66
  265.9 13.2 %shard_map.69 = f32[8,128]{1,0:T(8,128)} custom-call(f32[8,128]{1,0:T(8,128)} %pad_bitcast_fusion.3.x_ref), custom_call_target="tpu_custom_call" | custom-call | tf_op jit(solution)/shard_map/pallas_call | solution.py:66
  291.9 13.3 %all-gather.2 = f32[32,2,1024]{2,1,0:T(2,128)S(1)} all-gather(f32[4,2,1024]{2,1,0:T(2,128)S(1)} %copy.473), channel_id=4, replica_groups=mesh['brick'=8,'grp'=16] {'brick'}, dimensions={0}, use_global_device_ids=true | all-gather | bytes 294912 | tf_op jit(solution)/shard_map/all_gather | solution.py:192
  315.0 8.6 %multiply_divide_fusion.1 = (f32[2,32,32,32]{3,2,1,0:T(8,128)S(1)}, f32[2,32,32,32]{3,2,1,0:T(8,128)}) fusion(f32[2,32,32,32]{3,2,1,0:T(8,128)} %get-tuple-element.73, f32[2,32,32,32]{3,2,1,0:T(8,128)} %get-tuple-element.75, f32[2,32,32]{2,1,0:T(8,128)} %broadcast_in_dim.744, pred[32]{0:T(512)(128)(4,1)} %copy-done.97, ...), kind=kLoop, calls=%fused_computation.79 | loop fusion | flops 2097152 | bytes 4538476 | tf_op jit(solution)/shard_map/div | solution.py:307
  333.5 3.1 collective-permute-start.5
  340.5 3.0 pad_maximum_fusion.4
  345.9 3.0 fusion.96
  359.8 2.4 concatenate.751
  367.0 2.4 concatenate.705
  383.4 2.4 broadcast_in_dim.767
  385.9 3.7 multiply_reduce_fusion.3
  390.9 16.1 %shard_map.71 = f32[8,128]{1,0:T(8,128)} custom-call(f32[8,128]{1,0:T(8,128)} %pad_bitcast_fusion.2.x_ref), custom_call_target="tpu_custom_call" | custom-call | tf_op jit(solution)/shard_map/pallas_call | solution.py:66
  412.0 13.0 %all-gather.3 = f32[32,2,1024]{2,1,0:T(2,128)S(1)} all-gather(f32[4,2,1024]{2,1,0:T(2,128)S(1)} %copy.478), channel_id=5, replica_groups=mesh['brick'=8,'grp'=16] {'brick'}, dimensions={0}, use_global_device_ids=true | all-gather | bytes 294912 | tf_op jit(solution)/shard_map/all_gather | solution.py:192
  433.4 7.4 %multiply_add_fusion.1 = f32[2,32,32,32]{3,2,1,0:T(8,128)S(1)} fusion(f32[2,32,32,32]{3,2,1,0:T(8,128)S(1)} %get-tuple-element.63, f32[2,32,32,32]{3,2,1,0:T(8,128)} %get-tuple-element.73, f32[2,32,32,32]{3,2,1,0:T(8,128)} %get-tuple-element.59, f32[2,32,32,32]{3,2,1,0:T(8,128)} %get-tuple-element.75, f32[2,32,32,32]{3,2,1,0:T(8,128)} %get-tuple-element.74, ...), kind=kLoop, calls=%fused_computation.78 | loop fusion | flops 2359296 | bytes 4276340 | tf_op jit(solution)/shard_map/add | solution.py:345
  445.5 3.1 collective-permute-start.7
  449.9 2.7 pad_maximum_fusion.6
  454.0 2.5 broadcast_in_dim.783
  456.5 2.4 broadcast_in_dim.782
  466.7 2.5 concatenate.803
  476.7 2.5 broadcast_in_dim.778
  483.8 3.4 multiply_reduce_fusion.2
  488.8 16.3 %shard_map.72 = f32[8,128]{1,0:T(8,128)} custom-call(f32[8,128]{1,0:T(8,128)} %fusion.179.x_ref), custom_call_target="tpu_custom_call" | custom-call | tf_op jit(solution)/shard_map/pallas_call | solution.py:66
  511.5 12.8 %all-gather.4 = f32[32,2,1024]{2,1,0:T(2,128)S(1)} all-gather(f32[4,2,1024]{2,1,0:T(2,128)S(1)} %copy.483), channel_id=6, replica_groups=mesh['brick'=8,'grp'=16] {'brick'}, dimensions={0}, use_global_device_ids=true | all-gather | bytes 294912 | tf_op jit(solution)/shard_map/all_gather | solution.py:192
  532.8 8.0 %multiply_divide_fusion = f32[2,32,32,32]{3,2,1,0:T(8,128)S(1)} fusion(f32[2,32,32,32]{3,2,1,0:T(8,128)} %get-tuple-element.73, f32[2,32,32,32]{3,2,1,0:T(8,128)} %get-tuple-element.59, f32[2,32,32,32]{3,2,1,0:T(8,128)} %get-tuple-element.75, f32[2,32,32,32]{3,2,1,0:T(8,128)} %get-tuple-element.74, f32[2,32,32,32]{3,2,1,0:T(8,128)} %concatenate.766, ...), kind=kLoop, calls=%fused_computation.77 | loop fusion | flops 2031616 | bytes 4276332 | tf_op jit(solution)/shard_map/div | solution.py:307
  550.5 3.5 collective-permute-start.9
  556.7 3.0 pad_maximum_fusion.8
  564.1 2.4 broadcast_in_dim.800
  574.7 2.4 concatenate.816
  592.3 2.5 broadcast_in_dim.790
  598.3 2.4 broadcast_in_dim.787
  600.7 3.9 multiply_reduce_fusion.1
  605.7 16.3 %shard_map.73 = f32[8,128]{1,0:T(8,128)} custom-call(f32[8,128]{1,0:T(8,128)} %pad_bitcast_fusion.1.x_ref), custom_call_target="tpu_custom_call" | custom-call | tf_op jit(solution)/shard_map/pallas_call | solution.py:66
  633.9 12.8 %all-gather.5 = f32[32,2,1024]{2,1,0:T(2,128)S(1)} all-gather(f32[4,2,1024]{2,1,0:T(2,128)S(1)} %copy.488), channel_id=7, replica_groups=mesh['brick'=8,'grp'=16] {'brick'}, dimensions={0}, use_global_device_ids=true | all-gather | bytes 294912 | tf_op jit(solution)/shard_map/all_gather | solution.py:192
  656.1 10.7 %multiply_add_fusion = f32[2,32,32,32]{3,2,1,0:T(8,128)S(1)} fusion(f32[2,32,32,32]{3,2,1,0:T(8,128)} %copy-done.5, f32[2,32,32,32]{3,2,1,0:T(8,128)} %get-tuple-element.73, f32[2,32,32,32]{3,2,1,0:T(8,128)} %get-tuple-element.75, f32[2,32,32,32]{3,2,1,0:T(8,128)} %get-tuple-element.74, f32[2,32,32,32]{3,2,1,0:T(8,128)} %concatenate.784, ...), kind=kLoop, calls=%fused_computation.76 | loop fusion | flops 3735552 | bytes 5865592 | tf_op jit(solution)/shard_map/add | solution.py:345
  670.4 2.5 collective-permute-start.11
  685.6 2.4 concatenate.830
  688.0 2.4 concatenate.786
  698.3 2.5 broadcast_in_dim.804
  703.3 2.6 multiply_reduce_fusion
  707.5 16.9 %shard_map.74 = f32[8,128]{1,0:T(8,128)} custom-call(f32[8,128]{1,0:T(8,128)} %fusion.178.x_ref), custom_call_target="tpu_custom_call" | custom-call | tf_op jit(solution)/shard_map/pallas_call | solution.py:66
  726.8 6.0 fusion.148
  (747 shorter events, 353.0 us)
Async XLA Ops:
  0.6 9.8 %copy-start.37 = (f32[1,1,2,32,1024]{4,3,2,1,0:T(8,128)S(1)}, f32[1,1,2,32,1024]{4,3,2,1,0:T(8,128)}, u32[]{:S(2)}) copy-start(f32[1,1,2,32,1024]{4,3,2,1,0:T(8,128)} %param.10) | copy-start | bytes 786436
  0.6 11.1 %copy-start = (f32[1,1,6,2,32,1024]{5,4,3,2,1,0:T(8,128)S(1)}, f32[1,1,6,2,32,1024]{5,4,3,2,1,0:T(8,128)}, u32[]{:S(2)}) copy-start(f32[1,1,6,2,32,1024]{5,4,3,2,1,0:T(8,128)} %param.11) | copy-start | bytes 4718596
  4.7 35.3 %copy-start.97 = (pred[32]{0:T(512)(128)(4,1)}, pred[32]{0:T(512)(128)(4,1)S(1)}, u32[]{:S(2)}) copy-start(pred[32]{0:T(512)(128)(4,1)S(1)} %get-tuple-element.280) | copy-start | bytes 100
  4.7 35.3 %copy-start.103 = (pred[32]{0:T(512)(128)(4,1)}, pred[32]{0:T(512)(128)(4,1)S(1)}, u32[]{:S(2)}) copy-start(pred[32]{0:T(512)(128)(4,1)S(1)} %get-tuple-element.281) | copy-start | bytes 100
  8.1 31.9 %copy-start.87 = (f32[2]{0:T(128)}, f32[2]{0:T(128)S(1)}, u32[]{:S(2)}) copy-start(f32[2]{0:T(128)S(1)} %get-tuple-element.35) | copy-start | bytes 28
  15.3 6.9 copy-start.1
  21.9 5.9 copy-start.40
  22.1 5.8 copy-start.124
  22.1 5.7 copy-start.126
  22.1 5.7 copy-start.130
  22.1 5.7 copy-start.133
  22.2 17.8 %copy-start.121 = (f32[2]{0:T(128)}, f32[2]{0:T(128)S(1)}, u32[]{:S(2)}) copy-start(f32[2]{0:T(128)S(1)} %get-tuple-element.271) | copy-start | bytes 28
  27.9 11.2 %copy-start.22 = (f32[1,1,2,32,1024]{4,3,2,1,0:T(8,128)S(1)}, f32[1,1,2,32,1024]{4,3,2,1,0:T(8,128)}, u32[]{:S(2)}) copy-start(f32[1,1,2,32,1024]{4,3,2,1,0:T(8,128)} %param.9) | copy-start | bytes 786436
  30.5 88.9 %collective-permute-start.1 = (f32[1,2,1024]{2,1,0:T(2,128)}, f32[1,2,1024]{2,1,0:T(2,128)}, u32[]{:S(2)}, u32[]{:S(2)}) collective-permute-start(f32[1,2,1024]{2,1,0:T(2,128)} %stack_reshape_squeeze.37), channel_id=1, source_target_pairs={{0,1},{1,2},{2,3},{3,4},{4,5},{5,6},{6,7},{7,8},{8,9},{9,10},{10,1... | collective-permute-start | bytes 24584 | tf_op jit(solution)/shard_map/ppermute | solution.py:88
  35.6 82.9 %collective-permute-start = (f32[1,2,1024]{2,1,0:T(2,128)}, f32[1,2,1024]{2,1,0:T(2,128)}, u32[]{:S(2)}, u32[]{:S(2)}) collective-permute-start(f32[1,2,1024]{2,1,0:T(2,128)} %stack_reshape_squeeze.36), channel_id=1, source_target_pairs={{1,0},{2,1},{3,2},{4,3},{5,4},{6,5},{7,6},{8,7},{9,8},{10,9},{11,1... | collective-permute-start | bytes 24584 | tf_op jit(solution)/shard_map/ppermute | solution.py:91
  41.5 23.3 %copy-start.16 = (f32[2,32,1024]{2,1,0:T(8,128)}, f32[2,32,1024]{2,1,0:T(8,128)S(1)}, u32[]{:S(2)}) copy-start(f32[2,32,1024]{2,1,0:T(8,128)S(1)} %get-tuple-element.68) | copy-start | bytes 786436
  41.5 23.4 %copy-start.19 = (f32[2,32,1024]{2,1,0:T(8,128)}, f32[2,32,1024]{2,1,0:T(8,128)S(1)}, u32[]{:S(2)}) copy-start(f32[2,32,1024]{2,1,0:T(8,128)S(1)} %get-tuple-element.69) | copy-start | bytes 786436
  41.5 23.7 %copy-start.13 = (f32[2,32,1024]{2,1,0:T(8,128)}, f32[2,32,1024]{2,1,0:T(8,128)S(1)}, u32[]{:S(2)}) copy-start(f32[2,32,1024]{2,1,0:T(8,128)S(1)} %get-tuple-element.71) | copy-start | bytes 786436
  41.5 344.3 %copy-start.11 = (f32[2,32,1024]{2,1,0:T(8,128)}, f32[2,32,1024]{2,1,0:T(8,128)S(1)}, u32[]{:S(2)}) copy-start(f32[2,32,1024]{2,1,0:T(8,128)S(1)} %get-tuple-element.70) | copy-start | bytes 786436
  45.8 19.0 %copy-start.139 = (pred[8,4]{1,0:T(8,128)(4,1)}, pred[8,4]{1,0:T(8,128)(4,1)S(1)}, u32[]{:S(2)}) copy-start(pred[8,4]{1,0:T(8,128)(4,1)S(1)} %iota_compare_fusion.12) | copy-start | bytes 100
  65.8 24.4 %copy-start.7 = (f32[2,32,32,32]{3,2,1,0:T(8,128)S(1)}, f32[2,32,32,32]{3,2,1,0:T(8,128)}, u32[]{:S(2)}) copy-start(f32[2,32,32,32]{3,2,1,0:T(8,128)} %copy-done.6) | copy-start | bytes 786436
  90.1 14.9 %copy-start.57 = (f32[2,32,992]{2,1,0:T(8,128)S(1)}, f32[2,32,992]{2,1,0:T(8,128)}, u32[]{:S(2)}) copy-start(f32[2,32,992]{2,1,0:T(8,128)} %get-tuple-element.144) | copy-start | bytes 761860
  91.8 17.9 %copy-start.113 = (f32[1,2,1024]{2,1,0:T(2,128)S(1)}, f32[1,2,1024]{2,1,0:T(2,128)}, u32[]{:S(2)}) copy-start(f32[1,2,1024]{2,1,0:T(2,128)} %get-tuple-element.202) | copy-start | bytes 24580
  91.8 20.0 %copy-start.98 = (pred[32]{0:T(512)(128)(4,1)S(1)}, pred[32]{0:T(512)(128)(4,1)}, u32[]{:S(2)}) copy-start(pred[32]{0:T(512)(128)(4,1)} %copy-done.97) | copy-start | bytes 100
  91.8 20.7 %copy-start.104 = (pred[32]{0:T(512)(128)(4,1)S(1)}, pred[32]{0:T(512)(128)(4,1)}, u32[]{:S(2)}) copy-start(pred[32]{0:T(512)(128)(4,1)} %copy-done.103) | copy-start | bytes 100
  91.9 23.8 %copy-start.83 = (f32[2,32,32]{2,1,0:T(8,128)}, f32[2,32,32]{2,1,0:T(8,128)S(1)}, u32[]{:S(2)}) copy-start(f32[2,32,32]{2,1,0:T(8,128)S(1)} %reshape.2418) | copy-start | bytes 24580
  92.0 23.7 %copy-start.84 = (f32[2,32,32]{2,1,0:T(8,128)}, f32[2,32,32]{2,1,0:T(8,128)S(1)}, u32[]{:S(2)}) copy-start(f32[2,32,32]{2,1,0:T(8,128)S(1)} %reshape.2417) | copy-start | bytes 24580
  95.5 20.2 %copy-start.161 = (f32[32,1]{0,1:T(1,128)}, f32[32,1]{0,1:T(1,128)S(1)}, u32[]{:S(2)}) copy-start(f32[32,1]{0,1:T(1,128)S(1)} %reshape.2491) | copy-start | bytes 388
  105.2 10.7 %copy-start.55 = (f32[2,31,1024]{2,1,0:T(8,128)S(1)}, f32[2,31,1024]{2,1,0:T(8,128)}, u32[]{:S(2)}) copy-start(f32[2,31,1024]{2,1,0:T(8,128)} %get-tuple-element.140) | copy-start | bytes 761860
  106.4 13.7 %copy-start.166 = (f32[2]{0:T(128)}, f32[2]{0:T(128)S(1)}, u32[]{:S(2)}) copy-start(f32[2]{0:T(128)S(1)} %fusion.181) | copy-start | bytes 28
  175.9 45.6 %collective-permute-start.3 = (f32[1,2,1024]{2,1,0:T(2,128)}, f32[1,2,1024]{2,1,0:T(2,128)}, u32[]{:S(2)}, u32[]{:S(2)}) collective-permute-start(f32[1,2,1024]{2,1,0:T(2,128)} %stack_reshape_squeeze.39), channel_id=1, source_target_pairs={{0,1},{1,2},{2,3},{3,4},{4,5},{5,6},{6,7},{7,8},{8,9},{9,10},{10,1... | collective-permute-start | bytes 24584 | tf_op jit(solution)/shard_map/ppermute | solution.py:88
  179.1 50.8 %collective-permute-start.2 = (f32[1,2,1024]{2,1,0:T(2,128)}, f32[1,2,1024]{2,1,0:T(2,128)}, u32[]{:S(2)}, u32[]{:S(2)}) collective-permute-start(f32[1,2,1024]{2,1,0:T(2,128)} %stack_reshape_squeeze.38), channel_id=1, source_target_pairs={{1,0},{2,1},{3,2},{4,3},{5,4},{6,5},{7,6},{8,7},{9,8},{10,9},{11,1... | collective-permute-start | bytes 24584 | tf_op jit(solution)/shard_map/ppermute | solution.py:91
  289.8 19.6 %copy-start.36 = (f32[2,32,1024]{2,1,0:T(8,128)S(1)}, f32[2,32,1024]{2,1,0:T(8,128)}, u32[]{:S(2)}) copy-start(f32[2,32,1024]{2,1,0:T(8,128)} %copy-done.35) | copy-start | bytes 786436
  333.5 40.5 %collective-permute-start.5 = (f32[1,2,1024]{2,1,0:T(2,128)}, f32[1,2,1024]{2,1,0:T(2,128)}, u32[]{:S(2)}, u32[]{:S(2)}) collective-permute-start(f32[1,2,1024]{2,1,0:T(2,128)} %stack_reshape_squeeze.41), channel_id=1, source_target_pairs={{0,1},{1,2},{2,3},{3,4},{4,5},{5,6},{6,7},{7,8},{8,9},{9,10},{10,1... | collective-permute-start | bytes 24584 | tf_op jit(solution)/shard_map/ppermute | solution.py:88
  336.6 43.3 %collective-permute-start.4 = (f32[1,2,1024]{2,1,0:T(2,128)}, f32[1,2,1024]{2,1,0:T(2,128)}, u32[]{:S(2)}, u32[]{:S(2)}) collective-permute-start(f32[1,2,1024]{2,1,0:T(2,128)} %stack_reshape_squeeze.40), channel_id=1, source_target_pairs={{1,0},{2,1},{3,2},{4,3},{5,4},{6,5},{7,6},{8,7},{9,8},{10,9},{11,1... | collective-permute-start | bytes 24584 | tf_op jit(solution)/shard_map/ppermute | solution.py:91
  442.3 7.6 %copy-start.8 = (f32[2,32,32,31]{3,2,1,0:T(8,128)}, f32[2,32,32,31]{3,2,1,0:T(8,128)S(1)}, u32[]{:S(2)}) copy-start(f32[2,32,32,31]{3,2,1,0:T(8,128)S(1)} %get-tuple-element.90) | copy-start | bytes 761860
  442.3 7.6 %copy-start.151 = (f32[1,1,1024]{2,1,0:T(1,128)S(1)}, f32[1,1,1024]{2,1,0:T(1,128)}, u32[]{:S(2)}) copy-start(f32[1,1,1024]{2,1,0:T(1,128)} %get-tuple-element.242) | copy-start | bytes 12292
  442.3 7.6 %copy-start.154 = (f32[1,1,1024]{2,1,0:T(1,128)S(1)}, f32[1,1,1024]{2,1,0:T(1,128)}, u32[]{:S(2)}) copy-start(f32[1,1,1024]{2,1,0:T(1,128)} %get-tuple-element.190) | copy-start | bytes 12292
  445.5 28.5 %collective-permute-start.7 = (f32[1,2,1024]{2,1,0:T(2,128)}, f32[1,2,1024]{2,1,0:T(2,128)}, u32[]{:S(2)}, u32[]{:S(2)}) collective-permute-start(f32[1,2,1024]{2,1,0:T(2,128)} %stack_reshape_squeeze.43), channel_id=1, source_target_pairs={{0,1},{1,2},{2,3},{3,4},{4,5},{5,6},{6,7},{7,8},{8,9},{9,10},{10,1... | collective-permute-start | bytes 24584 | tf_op jit(solution)/shard_map/ppermute | solution.py:88
  448.6 30.7 %collective-permute-start.6 = (f32[1,2,1024]{2,1,0:T(2,128)}, f32[1,2,1024]{2,1,0:T(2,128)}, u32[]{:S(2)}, u32[]{:S(2)}) collective-permute-start(f32[1,2,1024]{2,1,0:T(2,128)} %stack_reshape_squeeze.42), channel_id=1, source_target_pairs={{1,0},{2,1},{3,2},{4,3},{5,4},{6,5},{7,6},{8,7},{9,8},{10,9},{11,1... | collective-permute-start | bytes 24584 | tf_op jit(solution)/shard_map/ppermute | solution.py:91
  454.0 10.3 %copy-start.27 = (f32[2,32,32,32]{3,2,1,0:T(8,128)S(1)}, f32[2,32,32,32]{3,2,1,0:T(8,128)}, u32[]{:S(2)}) copy-start(f32[2,32,32,32]{3,2,1,0:T(8,128)} %pad_maximum_fusion.6) | copy-start | bytes 786436
  476.7 7.1 copy-start.12
  476.7 7.1 copy-start.14
  476.7 7.1 copy-start.17
  476.7 7.1 copy-start.20
  483.8 25.1 %copy-start.46 = (f32[2,32,1024]{2,1,0:T(8,128)S(1)}, f32[2,32,1024]{2,1,0:T(8,128)}, u32[]{:S(2)}) copy-start(f32[2,32,1024]{2,1,0:T(8,128)} %get-tuple-element.57) | copy-start | bytes 786436
  487.3 37.1 %copy-start.140 = (pred[8,4]{1,0:T(8,128)(4,1)S(1)}, pred[8,4]{1,0:T(8,128)(4,1)}, u32[]{:S(2)}) copy-start(pred[8,4]{1,0:T(8,128)(4,1)} %copy-done.139) | copy-start | bytes 100
  550.5 38.3 %collective-permute-start.9 = (f32[1,2,1024]{2,1,0:T(2,128)}, f32[1,2,1024]{2,1,0:T(2,128)}, u32[]{:S(2)}, u32[]{:S(2)}) collective-permute-start(f32[1,2,1024]{2,1,0:T(2,128)} %stack_reshape_squeeze.45), channel_id=1, source_target_pairs={{0,1},{1,2},{2,3},{3,4},{4,5},{5,6},{6,7},{7,8},{8,9},{9,10},{10,1... | collective-permute-start | bytes 24584 | tf_op jit(solution)/shard_map/ppermute | solution.py:88
  554.0 40.8 %collective-permute-start.8 = (f32[1,2,1024]{2,1,0:T(2,128)}, f32[1,2,1024]{2,1,0:T(2,128)}, u32[]{:S(2)}, u32[]{:S(2)}) collective-permute-start(f32[1,2,1024]{2,1,0:T(2,128)} %stack_reshape_squeeze.44), channel_id=1, source_target_pairs={{1,0},{2,1},{3,2},{4,3},{5,4},{6,5},{7,6},{8,7},{9,8},{10,9},{11,1... | collective-permute-start | bytes 24584 | tf_op jit(solution)/shard_map/ppermute | solution.py:91
  592.3 8.4 %copy-start.91 = (f32[2]{0:T(128)S(1)}, f32[2]{0:T(128)}, u32[]{:S(2)}) copy-start(f32[2]{0:T(128)} %copy-done.87) | copy-start | bytes 28
  592.3 8.4 %copy-start.110 = (pred[1024]{0:T(1024)(128)(4,1)S(1)}, pred[1024]{0:T(1024)(128)(4,1)}, u32[]{:S(2)}) copy-start(pred[1024]{0:T(1024)(128)(4,1)} %broadcast_in_dim.716) | copy-start | bytes 3076
  592.3 8.4 %copy-start.112 = (pred[1024]{0:T(1024)(128)(4,1)S(1)}, pred[1024]{0:T(1024)(128)(4,1)}, u32[]{:S(2)}) copy-start(pred[1024]{0:T(1024)(128)(4,1)} %broadcast_in_dim.698) | copy-start | bytes 3076
  592.3 8.4 %copy-start.123 = (f32[2]{0:T(128)S(1)}, f32[2]{0:T(128)}, u32[]{:S(2)}) copy-start(f32[2]{0:T(128)} %copy-done.121) | copy-start | bytes 28
  604.6 42.1 %copy-start.141 = (pred[8,4]{1,0:T(8,128)(4,1)S(1)}, pred[8,4]{1,0:T(8,128)(4,1)}, u32[]{:S(2)}) copy-start(pred[8,4]{1,0:T(8,128)(4,1)} %copy-done.139) | copy-start | bytes 100
  626.8 23.4 %copy-start.25 = (f32[2,32,1024]{2,1,0:T(8,128)S(1)}, f32[2,32,1024]{2,1,0:T(8,128)}, u32[]{:S(2)}) copy-start(f32[2,32,1024]{2,1,0:T(8,128)} %copy-done.24) | copy-start | bytes 786436
  668.4 6.0 copy-start.146
  668.4 6.0 copy-start.149
  670.4 23.6 %collective-permute-start.11 = (f32[1,2,1024]{2,1,0:T(2,128)S(1)}, f32[1,2,1024]{2,1,0:T(2,128)S(1)}, u32[]{:S(2)}, u32[]{:S(2)}) collective-permute-start(f32[1,2,1024]{2,1,0:T(2,128)S(1)} %stack_reshape_squeeze.47), channel_id=1, source_target_pairs={{0,1},{1,2},{2,3},{3,4},{4,5},{5,6},{6,7},{7,8},{8,9},{9,10},{10,1... | collective-permute-start | bytes 24584 | tf_op jit(solution)/shard_map/ppermute | solution.py:88
  673.0 23.9 %collective-permute-start.10 = (f32[1,2,1024]{2,1,0:T(2,128)S(1)}, f32[1,2,1024]{2,1,0:T(2,128)S(1)}, u32[]{:S(2)}, u32[]{:S(2)}) collective-permute-start(f32[1,2,1024]{2,1,0:T(2,128)S(1)} %stack_reshape_squeeze.46), channel_id=1, source_target_pairs={{1,0},{2,1},{3,2},{4,3},{5,4},{6,5},{7,6},{8,7},{9,8},{10,9},{11,1... | collective-permute-start | bytes 24584 | tf_op jit(solution)/shard_map/ppermute | solution.py:91
  703.3 23.4 %copy-start.39 = (f32[1,1,2,32,1024]{4,3,2,1,0:T(8,128)S(1)}, f32[1,1,2,32,1024]{4,3,2,1,0:T(8,128)}, u32[]{:S(2)}) copy-start(f32[1,1,2,32,1024]{4,3,2,1,0:T(8,128)} %param.10) | copy-start | bytes 786436
  703.3 23.4 %copy-start.73 = (pred[32,1024]{1,0:T(8,128)(4,1)S(1)}, pred[32,1024]{1,0:T(8,128)(4,1)}, u32[]{:S(2)}) copy-start(pred[32,1024]{1,0:T(8,128)(4,1)} %copy-done.71) | copy-start | bytes 98308
  703.3 23.4 %copy-start.76 = (pred[32,1024]{1,0:T(8,128)(4,1)S(1)}, pred[32,1024]{1,0:T(8,128)(4,1)}, u32[]{:S(2)}) copy-start(pred[32,1024]{1,0:T(8,128)(4,1)} %copy-done.74) | copy-start | bytes 98308
  726.8 6.1 copy-start.54
  726.8 6.1 copy-start.156
  (126 other events, 367.7 us)
